TPU v7x, 32 devices: a whole 2x2x4 slice. The times are simulated.
32 devices in a mesh: shard: 4 (over z), tensor: 4 (over x, core), section: 2 (over y).
Axes of the slice: x: 2, y: 2, z: 4, core: 2. Of those that a mesh axis runs over, the one named last changes fastest.
Arguments:
- hidden_acts: bfloat16 [2, 10240, 4096], P('section', 'shard', 'tensor'), may hold values from -8 to 8
- out_grads: bfloat16 [2, 10240, 1024], P('section', 'shard'), may hold values from -8 to 8
- errors: float32 [2, 4, 1024, 4096], P('section', 'shard', None, 'tensor'), may hold values from -3 to 3
- factors: float32 [2, 32, 4096], P('section', None, 'tensor'), may hold values from -6 to 6
- whiten: float32 [2, 2, 32, 32], P('section'), may hold values from -1.5 to 3
- momentum: float32 [2, 1024, 4096], P('section', 'shard', 'tensor'), may hold values from -3 to 3
- master: float32 [2, 1024, 4096], P('section', 'shard', 'tensor'), may hold values from -3 to 3
- table: bfloat16 [32768, 1024], P(('shard', 'section'), 'tensor'), may hold values from -5 to 5
- touched_ids: int32 [1024], P(('shard', 'section')), may hold values from 0 to 32767, as said below
- touched_grads: bfloat16 [1024, 1024], P(('shard', 'section'), 'tensor'), may hold values from -5 to 5
Outputs:
- new_errors: float32 [2, 4, 1024, 4096], P('section', 'shard', None, 'tensor')
- new_factors: float32 [2, 32, 4096], P('section', None, 'tensor')
- new_momentum: float32 [2, 1024, 4096], P('section', 'shard', 'tensor')
- new_master: float32 [2, 1024, 4096], P('section', 'shard', 'tensor')
- new_weights: bfloat16 [2, 1024, 4096], P('section', None, 'tensor')
- new_table: bfloat16 [32768, 1024], P(('shard', 'section'), 'tensor')
Inputs may be any that keep to these rules, and one draw needn't show every extreme that they name: `touched_ids`: the 128 ids of one device of shard and section name at most 32 rows in each block of 4096 vocabulary rows; in every draw one block receives exactly 32 rows from every device.
All inputs are finite; a program needn't handle non-finite values.
Results may differ from a plain program's by a relative error of at most 0.0036.
Values may be sent and summed in bfloat16 or wider, within the bound.
A program may use at most 128 MiB of HBM per device.

v0:
```python
import jax
import jax.numpy as jnp
from jax import lax
from jax.sharding import PartitionSpec as P

D = 1024
FF = 4096
ROUNDS = 2


epsilon = 1e-06
momentum_decay = 0.9
learn_rate = 0.1
embed_rate = 0.25
clip_level = 0.03
highest = lax.Precision.HIGHEST


def on_device(
    hidden_acts,
    out_grads,
    errors,
    factors,
    whiten,
    momentum,
    master,
    table,
    touched_ids,
    touched_grads,
):
    shards = lax.axis_size("shard")
    grad_block = lax.dot_general(
        out_grads[0], hidden_acts[0], (((0,), (0,)), ((), ())), preferred_element_type=jnp.float32
    )
    rounded = lax.optimization_barrier(grad_block.astype(jnp.bfloat16))
    corrected = rounded.astype(jnp.float32) + errors[0, 0]
    right_part = factors[0]
    rank_count = right_part.shape[0]
    left_unit = None
    for power_round in range(ROUNDS):
        left_part = lax.dot_general(
            right_part,
            corrected,
            (((1,), (1,)), ((), ())),
            precision=highest,
            preferred_element_type=jnp.float32,
        )
        left_sum = lax.psum(left_part, ("shard", "tensor"))
        whitened = jnp.dot(whiten[0, power_round].T, left_sum, precision=highest)
        scaling = lax.rsqrt(jnp.sum(whitened * whitened) / rank_count + epsilon)
        left_unit = whitened * scaling
        right_local = jnp.dot(left_unit, corrected, precision=highest)
        right_part = lax.psum(right_local, "shard") / shards
    gram_left = jnp.dot(left_unit, left_unit.T, precision=highest)
    gram_right = jnp.dot(right_part, right_part.T, precision=highest)
    total_squares = lax.psum(jnp.sum(gram_left * gram_right), ("tensor", "section"))
    approx = lax.dot_general(
        left_unit,
        right_part,
        (((0,), (0,)), ((), ())),
        precision=highest,
        preferred_element_type=jnp.float32,
    )
    new_errors = (corrected - approx)[None, None]
    entries = lax.axis_size("section") * D * FF
    spread = jnp.sqrt(total_squares / entries + epsilon)
    clip_factor = jnp.minimum(1.0, clip_level / spread)
    rows_own = momentum.shape[1]
    row_start = lax.axis_index("shard") * rows_own
    approx_rows = lax.dynamic_slice_in_dim(approx, row_start, rows_own, 0)
    new_momentum = momentum_decay * momentum + clip_factor * approx_rows[None]
    new_master = master - learn_rate * new_momentum
    new_weights = lax.all_gather(new_master.astype(jnp.bfloat16), "shard", axis=1, tiled=True)
    new_factors = right_part[None]
    vocab_rows = table.shape[0]
    table_width = table.shape[1]
    first_row = lax.axis_index(("shard", "section")) * vocab_rows
    recv_rows, recv_ids = (
        lax.all_gather(touched_grads, ("shard", "section"), axis=0, tiled=True),
        lax.all_gather(touched_ids, ("shard", "section"), axis=0, tiled=True),
    )
    local_index = recv_ids - first_row
    inside = (local_index >= 0) & (local_index < vocab_rows)
    target = jnp.where(inside, local_index, vocab_rows)
    table_grad = (
        jnp.zeros((vocab_rows, table_width), jnp.float32)
        .at[target]
        .add(recv_rows.astype(jnp.float32), mode="drop")
    )
    new_table = (table.astype(jnp.float32) - embed_rate * table_grad).astype(jnp.bfloat16)
    return (new_errors, new_factors, new_momentum, new_master, new_weights, new_table)


def solution(mesh):
    in_specs = (
        P("section", "shard", "tensor"),
        P("section", "shard", None),
        P("section", "shard", None, "tensor"),
        P("section", None, "tensor"),
        P("section", None, None, None),
        P("section", "shard", "tensor"),
        P("section", "shard", "tensor"),
        P(("shard", "section"), "tensor"),
        P(("shard", "section")),
        P(("shard", "section"), "tensor"),
    )
    out_specs = (
        P("section", "shard", None, "tensor"),
        P("section", None, "tensor"),
        P("section", "shard", "tensor"),
        P("section", "shard", "tensor"),
        P("section", None, "tensor"),
        P(("shard", "section"), "tensor"),
    )
    return jax.shard_map(
        on_device, mesh=mesh, in_specs=in_specs, out_specs=out_specs, check_vma=False
    )
```

profile of v0, /device:TPU:0, one launch (start us, length us, event | category | flops | bytes accessed | tf_op | source)
XLA Modules:
  0.0 398.0 jit_solution(17824651592674097183)
XLA Ops:
  7.2 9.3 %fusion.5 = bf16[1024,1024]{1,0:T(8,128)(2,1)S(1)} fusion(bf16[1,2560,1024]{2,1,0:T(8,128)(2,1)} %param.10, bf16[1,2560,1024]{2,1,0:T(8,128)(2,1)} %param.11), kind=kOutput, calls=%fused_computation.9 | convolution fusion | flops 5369757696 | bytes 12582912 | tf_op jit(solution)/shard_map/dot_general | solution.py:32
  16.6 4.7 %convolution_bitcast_fusion = f32[32,1024]{1,0:T(8,128)} fusion(f32[1,32,1024]{2,1,0:T(8,128)S(1)} %copy-done, f32[1,1,1024,1024]{3,2,1,0:T(8,128)S(1)} %copy-done.1, bf16[1024,1024]{1,0:T(8,128)(2,1)S(1)} %fusion.5), kind=kOutput, calls=%fused_computation.10 | convolution fusion | flops 404750336 | bytes 6553600 | tf_op jit(solution)/shard_map/dot_general | solution.py:41
  21.3 89.8 %all-reduce.5.cloned.1.call-done = f32[32,1024]{1,0:T(8,128)} async-done(((f32[32,1024]{1,0:T(8,128)}), f32[32,1024]{1,0:T(8,128)}) %all-reduce.5.cloned.1.call-update) | async-done | bytes 131088 | tf_op jit(solution)/shard_map/psum | solution.py:48
  111.1 1.8 multiply_reduce_fusion.1
  113.7 5.6 %fusion.15 = f32[32,1024]{1,0:T(8,128)} fusion(f32[1024,32]{0,1:T(8,128)S(1)} %get-tuple-element.10, f32[]{:T(128)S(6)} %rsqrt.7, f32[1,1,1024,1024]{3,2,1,0:T(8,128)} %param.12, bf16[1024,1024]{1,0:T(8,128)(2,1)S(1)} %fusion.5), kind=kOutput, calls=%fused_computation.20 | convolution fusion | flops 404783104 | bytes 6553604 | tf_op jit(solution)/shard_map/dot_general | solution.py:52
  119.3 36.2 %all-reduce.7.cloned.1.call-done = f32[32,1024]{1,0:T(8,128)} async-done(((f32[32,1024]{1,0:T(8,128)}), f32[32,1024]{1,0:T(8,128)}) %all-reduce.7.cloned.1.call-update) | async-done | bytes 131088 | tf_op jit(solution)/shard_map/psum | solution.py:53
  155.5 6.8 %fusion.13 = f32[32,1024]{1,0:T(8,128)} fusion(f32[32,1024]{1,0:T(8,128)} %all-reduce.7.cloned.1.call-done, f32[1,1,1024,1024]{3,2,1,0:T(8,128)} %param.12, bf16[1024,1024]{1,0:T(8,128)(2,1)S(1)} %fusion.5), kind=kOutput, calls=%fused_computation.18 | convolution fusion | flops 404783104 | bytes 6553600 | tf_op jit(solution)/shard_map/dot_general | solution.py:41
  162.5 86.6 %all-reduce.9.cloned.1.call-done = f32[32,1024]{1,0:T(8,128)} async-done(((f32[32,1024]{1,0:T(8,128)}), f32[32,1024]{1,0:T(8,128)}) %all-reduce.9.cloned.1.call-update) | async-done | bytes 131088 | tf_op jit(solution)/shard_map/psum | solution.py:48
  249.1 1.8 multiply_reduce_fusion
  251.6 5.6 %fusion.23 = f32[32,1024]{1,0:T(8,128)} fusion(f32[1024,32]{0,1:T(8,128)S(1)} %get-tuple-element.12, f32[]{:T(128)S(6)} %rsqrt.8, f32[1,1,1024,1024]{3,2,1,0:T(8,128)} %param.12, bf16[1024,1024]{1,0:T(8,128)(2,1)S(1)} %fusion.5), kind=kOutput, calls=%fused_computation.30 | convolution fusion | flops 404783104 | bytes 6553604 | tf_op jit(solution)/shard_map/dot_general | solution.py:52
  257.6 36.0 %all-reduce.11.cloned.1.call-done = f32[32,1024]{1,0:T(8,128)} async-done(((f32[32,1024]{1,0:T(8,128)}), f32[32,1024]{1,0:T(8,128)}) %all-reduce.11.cloned.1.call-update) | async-done | bytes 131088 | tf_op jit(solution)/shard_map/psum | solution.py:53
  293.6 1.8 fusion.11
  295.4 14.0 %psum.39 = f32[]{:T(128)} all-reduce(f32[]{:T(128)} %fusion.11), channel_id=1, replica_groups=mesh['shard'=4,'tensor'=4,'section'=2] {'tensor','section'}, use_global_device_ids=true, to_apply=%region_7.0 | all-reduce | flops 1 | bytes 8 | tf_op jit(solution)/shard_map/psum | solution.py:56
  310.1 4.5 %fusion.18 = f32[1024,1024]{1,0:T(8,128)S(1)} fusion(f32[32,1024]{1,0:T(8,128)} %all-reduce.11.cloned.1.call-done, f32[1024,32]{0,1:T(8,128)S(1)} %get-tuple-element.12, f32[]{:T(128)S(6)} %rsqrt.8), kind=kOutput, calls=%fused_computation.25 | convolution fusion | flops 402718720 | bytes 4456452 | tf_op jit(solution)/shard_map/dot_general | solution.py:57
  314.6 2.0 copy-done.3
  316.6 1.9 fusion.41
  318.6 18.6 %all-gather = s32[8,1,128]{2,1,0:T(1,128)S(1)} all-gather(s32[1,1,128]{2,1,0:T(1,128)S(1)} %bitcast.48), channel_id=1, replica_groups=mesh['shard'=4,'tensor'=4,'section'=2] {'shard','section'}, dimensions={0}, use_global_device_ids=true | all-gather | bytes 4608 | tf_op jit(solution)/shard_map/all_gather | solution.py:80
  337.2 33.2 %all_gather.11 = bf16[1024,256]{1,0:T(8,128)(2,1)S(1)} all-gather(bf16[128,256]{1,0:T(8,128)(2,1)S(1)} %copy-done.8), channel_id=1, replica_groups=mesh['shard'=4,'tensor'=4,'section'=2] {'shard','section'}, dimensions={0}, use_global_device_ids=true | all-gather | bytes 589824 | tf_op jit(solution)/shard_map/all_gather | solution.py:79
  370.3 8.3 %scatter_custom_fusion = f32[4096,256]{1,0:T(8,128)} fusion(s32[1024]{0:T(1024)S(1)} %compare_select_fusion, f32[]{:T(128)} %constant.16.clone.1, bf16[1024,256]{1,0:T(8,128)(2,1)S(1)} %all_gather.11), kind=kCustom, calls=%fused_computation.7 | custom fusion | flops 524288 | bytes 4718596 | tf_op jit(solution)/shard_map/scatter-add | solution.py:88
  378.6 4.8 %subtract_convert_fusion = bf16[4096,256]{1,0:T(8,128)(2,1)} fusion(f32[4096,256]{1,0:T(8,128)} %scatter_custom_fusion, bf16[4096,256]{1,0:T(8,128)(2,1)} %param.17), kind=kLoop, calls=%fused_computation.5 | loop fusion | flops 4194304 | bytes 8388608 | tf_op jit(solution)/shard_map/convert_element_type | solution.py:90
  383.4 0.7 multiply_bitcast_fusion
  384.1 0.6 copy-done.4
  384.7 3.6 subtract_bitcast_fusion
  388.3 3.1 copy.21
  (34 shorter events, 0.8 us)
Async XLA Ops:
  7.2 9.4 %copy-start = (f32[1,32,1024]{2,1,0:T(8,128)S(1)}, f32[1,32,1024]{2,1,0:T(8,128)}, u32[]{:S(2)}) copy-start(f32[1,32,1024]{2,1,0:T(8,128)} %param.13) | copy-start | bytes 393220
  7.2 103.9 %all-reduce.5.cloned.1.call-start = ((), (), s32[]{:S(2)}) async-start(), calls=%async_computation | async-start | bytes 262144 | tf_op jit(solution)/shard_map/psum | solution.py:48
  7.2 9.3 %copy-start.1 = (f32[1,1,1024,1024]{3,2,1,0:T(8,128)S(1)}, f32[1,1,1024,1024]{3,2,1,0:T(8,128)}, u32[]{:S(2)}) copy-start(f32[1,1,1024,1024]{3,2,1,0:T(8,128)} %param.12) | copy-start | bytes 12582916
  16.5 94.6 %copy-start.9 = (f32[1,2,32,32]{3,2,1,0:T(8,128)S(1)}, f32[1,2,32,32]{3,2,1,0:T(8,128)}, u32[]{:S(2)}) copy-start(f32[1,2,32,32]{3,2,1,0:T(8,128)} %param.14) | copy-start | bytes 24580
  21.3 134.2 %all-reduce.7.cloned.1.call-start = ((), (), s32[]{:S(2)}) async-start(), calls=%async_computation.1 | async-start | bytes 262144 | tf_op jit(solution)/shard_map/psum | solution.py:53
  119.2 129.8 %all-reduce.9.cloned.1.call-start = ((), (), s32[]{:S(2)}) async-start(), calls=%async_computation.2 | async-start | bytes 262144 | tf_op jit(solution)/shard_map/psum | solution.py:48
  162.3 131.3 %all-reduce.11.cloned.1.call-start = ((), (), s32[]{:S(2)}) async-start(), calls=%async_computation.3 | async-start | bytes 262144 | tf_op jit(solution)/shard_map/psum | solution.py:53
  251.6 65.0 %copy-start.6 = (f32[1,256,1024]{2,1,0:T(8,128)S(1)}, f32[1,256,1024]{2,1,0:T(8,128)}, u32[]{:S(2)}) copy-start(f32[1,256,1024]{2,1,0:T(8,128)} %param.16) | copy-start | bytes 3145732
  257.3 131.1 %all-gather.3.cloned.1.call-start = ((), (), s32[]{:S(2)}) async-start(), calls=%async_computation.4 | async-start | bytes 2621440 | tf_op jit(solution)/shard_map/all_gather | solution.py:73
  310.1 6.5 %copy-start.7 = (f32[1,256,1024]{2,1,0:T(8,128)S(1)}, f32[1,256,1024]{2,1,0:T(8,128)}, u32[]{:S(2)}) copy-start(f32[1,256,1024]{2,1,0:T(8,128)} %param.15) | copy-start | bytes 3145732
  314.6 2.0 copy-start.3
  316.6 2.0 copy-start.10
  316.6 20.6 %copy-start.8 = (bf16[128,256]{1,0:T(8,128)(2,1)S(1)}, bf16[128,256]{1,0:T(8,128)(2,1)}, u32[]{:S(2)}) copy-start(bf16[128,256]{1,0:T(8,128)(2,1)} %param.19) | copy-start | bytes 196612
  370.3 13.1 %copy-start.5 = (f32[32,1024]{1,0:T(8,128)S(1)}, f32[32,1024]{1,0:T(8,128)}, u32[]{:S(2)}) copy-start(f32[32,1024]{1,0:T(8,128)} %all-reduce.11.cloned.1.call-done) | copy-start | bytes 393220
  378.6 5.5 %copy-start.2 = (f32[1,1,1024,1024]{3,2,1,0:T(8,128)S(1)}, f32[1,1,1024,1024]{3,2,1,0:T(8,128)}, u32[]{:S(2)}) copy-start(f32[1,1,1024,1024]{3,2,1,0:T(8,128)} %param.12) | copy-start | bytes 12582916
  378.6 6.1 %copy-start.4 = (f32[1024,1024]{1,0:T(8,128)S(1)}, f32[1024,1024]{1,0:T(8,128)}, u32[]{:S(2)}) copy-start(f32[1024,1024]{1,0:T(8,128)} %copy-done.3) | copy-start | bytes 12582916
Sparse Core Ops, SparseCore 0:
  21.4 89.6 all-reduce.4
  119.4 36.0 all-reduce.6
  162.4 86.6 all-reduce.8
  257.4 36.1 all-reduce.10
  318.7 49.5 all-gather.2
where the time goes:
time: 398 us
  waiting for transfers between devices  249 us (63%)
  blocking collectives  65.7 us (17%)
  matrix products  42.2 us (11%)
  other arithmetic  19.3 us (5%)
  between operations  16 us (4%)
  local copies, waits for them, and re-layouts  5.77 us (1%)
    psum x2, waiting for transfers between devices, on_device(): left_sum = lax.psum(left_part, ('shard', 'tensor'))  176 us
    psum x2, waiting for transfers between devices, on_device(): right_part = lax.psum(right_local, 'shard') / shards  72.2 us
    all_gather x1, blocking collectives, on_device(): lax.all_gather(touched_grads, ('shard', 'section'), axis=0, tiled=True)  33.2 us
    all_gather x1, blocking collectives, on_device(): lax.all_gather(touched_ids, ('shard', 'section'), axis=0, tiled=True)  18.6 us
    psum x1, blocking collectives, on_device(): lax.psum(jnp.sum(gram_left * gram_right), ('tensor', 'section'))  14 us
    dot_general x2, matrix products, on_device(): lax.dot_general(right_part, corrected, (((1,), (1,)), ((), ())), precisio...  11.4 us
    dot_general x2, matrix products, on_device(): right_local = jnp.dot(left_unit, corrected, precision=highest)  11.2 us
    dot_general x1, matrix products, on_device(): lax.dot_general(out_grads[0], hidden_acts[0], (((0,), (0,)), ((), ())), p...  9.28 us
  transfers between devices with their start and end apart: 5, of which 4 were waited for; matrix products, arithmetic and copies ran while one was open for 4% of the time, Pallas kernels for 0%

commit v1 on v0

v1 whole, which is shorter than its diff:
```python
import functools

import jax
import jax.numpy as jnp
from jax import lax
from jax.experimental import pallas as pl
from jax.experimental.pallas import tpu as pltpu
from jax.sharding import PartitionSpec as P

ROUNDS = 2
LANES = 128

epsilon = 1e-06
momentum_decay = 0.9
learn_rate = 0.1
embed_rate = 0.25
clip_level = 0.03
highest = lax.Precision.HIGHEST
f32 = jnp.float32
bf16 = jnp.bfloat16
MESH = pl.DeviceIdType.MESH


def split(x):
    high = x.astype(bf16)
    low = (x - high.astype(f32)).astype(bf16)
    return high, low


def pieces(rank, width, count):
    rows = rank * (width // LANES) // count
    step = min(rows, rank)
    out = []
    for g in range(count):
        parts = []
        for at in range(0, rows, step):
            flat = g * rows + at
            parts.append((at, flat % rank, flat // rank * LANES, step))
        out.append(parts)
    return rows, out


def power_kernel(
    sizes,
    corrected_ref,
    factors_ref,
    whiten_ref,
    left_ref,
    right_ref,
    total_ref,
    high_ref,
    low_ref,
    lsend,
    lrecv,
    lgath,
    rsend,
    rrecv,
    rgath,
    square,
    full,
    lsem,
    rsem,
    qsem,
):
    shards, tensors, sections = sizes
    rank = factors_ref.shape[0]
    shard = lax.axis_index("shard")
    tensor = lax.axis_index("tensor")
    section = lax.axis_index("section")
    group = shards * tensors
    me = shard * tensors + tensor

    def left_peer(k):
        index = lax.rem(me + k, group)
        return index, {"shard": index // tensors, "tensor": lax.rem(index, tensors)}

    def right_peer(k):
        index = lax.rem(shard + k, shards)
        return index, {"shard": index}

    me_square = section * tensors + tensor
    squares = sections * tensors

    def square_peer(k):
        index = lax.rem(me_square + k, squares)
        return index, {"section": index // tensors, "tensor": lax.rem(index, tensors)}

    barrier = pltpu.get_barrier_semaphore()

    @pl.loop(1, group)
    def _(k):
        pl.semaphore_signal(barrier, inc=1, device_id=left_peer(k)[1], device_id_type=MESH)

    for other in range(1, sections):
        for t in range(tensors):
            there = {"section": lax.rem(section + other, sections), "tensor": t}
            pl.semaphore_signal(barrier, inc=1, device_id=there, device_id_type=MESH)

    high, low = split(corrected_ref[...])
    high_ref[...] = high
    low_ref[...] = low
    pl.semaphore_wait(barrier, group - 1 + (sections - 1) * tensors)

    def exchange(count, copy):
        @pl.loop(1, count)
        def _(k):
            copy(k).start()

        @pl.loop(1, count)
        def _(k):
            copy(k).wait()

    def all_reduce(value, count, own, peer, send, recv, gath, sems):
        rows, cuts = pieces(value.shape[0], value.shape[1], count)
        for g in range(count):
            for at, row, col, step in cuts[g]:
                send[g, at : at + step, :] = value[row : row + step, col : col + LANES]

        def scatter(k):
            index, there = peer(k)
            return pltpu.make_async_remote_copy(
                src_ref=send.at[index],
                dst_ref=recv.at[k],
                send_sem=sems.at[0, k],
                recv_sem=sems.at[1, k],
                device_id=there,
                device_id_type=MESH,
            )

        exchange(count, scatter)
        total = send[own]
        for k in range(1, count):
            total = total + recv[k]
        gath[own] = total

        def gather(k):
            _, there = peer(k)
            return pltpu.make_async_remote_copy(
                src_ref=gath.at[own],
                dst_ref=gath.at[own],
                send_sem=sems.at[2, k],
                recv_sem=sems.at[3, k],
                device_id=there,
                device_id_type=MESH,
            )

        exchange(count, gather)
        for g in range(count):
            for at, row, col, step in cuts[g]:
                full[row : row + step, col : col + LANES] = gath[g, at : at + step, :]
        return full[...]

    def times(x, dims):
        x_high, x_low = split(x)
        both = jnp.concatenate([x_high, x_low], axis=0)
        first = lax.dot_general(both, high_ref[...], (dims, ((), ())), preferred_element_type=f32)
        second = lax.dot_general(x_high, low_ref[...], (dims, ((), ())), preferred_element_type=f32)
        return first[:rank] + (first[rank:] + second)

    right = factors_ref[...]
    left_unit = None
    for turn in range(ROUNDS):
        left_part = times(right, ((1,), (1,)))
        left = all_reduce(
            left_part, group, me, left_peer, lsend.at[turn], lrecv.at[turn], lgath.at[turn], lsem.at[turn]
        )
        whitened = lax.dot_general(
            whiten_ref[turn], left, (((0,), (0,)), ((), ())), precision=highest, preferred_element_type=f32
        )
        left_unit = whitened * lax.rsqrt(jnp.sum(whitened * whitened) / rank + epsilon)
        right_part = times(left_unit, ((1,), (0,)))
        right = all_reduce(
            right_part, shards, shard, right_peer, rsend.at[turn], rrecv.at[turn], rgath.at[turn], rsem.at[turn]
        ) * (1.0 / shards)

    right_ref[...] = right
    last = (((1,), (1,)), ((), ()))
    gram_left = lax.dot_general(left_unit, left_unit, last, precision=highest, preferred_element_type=f32)
    gram_right = lax.dot_general(right, right, last, precision=highest, preferred_element_type=f32)
    square[0] = jnp.full(square.shape[1:], jnp.sum(gram_left * gram_right), f32)

    def share(k):
        _, there = square_peer(k)
        return pltpu.make_async_remote_copy(
            src_ref=square.at[0],
            dst_ref=square.at[k],
            send_sem=qsem.at[0, k],
            recv_sem=qsem.at[1, k],
            device_id=there,
            device_id_type=MESH,
        )

    @pl.loop(1, squares)
    def _(k):
        share(k).start()

    left_high = left_unit.astype(bf16).astype(f32)
    stacked = jnp.concatenate([left_high, left_unit - left_high, left_high], axis=0)
    left_ref[...] = stacked.T.astype(bf16)

    @pl.loop(1, squares)
    def _(k):
        share(k).wait()

    total = square[0]
    for k in range(1, squares):
        total = total + square[k]
    total_ref[...] = total


def run_power(sizes, corrected, factors, whiten):
    shards, tensors, sections = sizes
    rank, width = factors.shape
    depth = corrected.shape[0]
    group = shards * tensors
    left_rows = rank * (depth // LANES) // group
    right_rows = rank * (width // LANES) // shards
    vmem = pl.BlockSpec(memory_space=pltpu.VMEM)
    return pl.pallas_call(
        functools.partial(power_kernel, sizes),
        out_shape=(
            jax.ShapeDtypeStruct((depth, 3 * rank), bf16),
            jax.ShapeDtypeStruct((rank, width), f32),
            jax.ShapeDtypeStruct((8, LANES), f32),
        ),
        in_specs=[vmem] * 3,
        out_specs=(vmem,) * 3,
        scratch_shapes=[
            pltpu.VMEM((depth, width), bf16),
            pltpu.VMEM((depth, width), bf16),
            pltpu.VMEM((ROUNDS, group, left_rows, LANES), f32),
            pltpu.VMEM((ROUNDS, group, left_rows, LANES), f32),
            pltpu.VMEM((ROUNDS, group, left_rows, LANES), f32),
            pltpu.VMEM((ROUNDS, shards, right_rows, LANES), f32),
            pltpu.VMEM((ROUNDS, shards, right_rows, LANES), f32),
            pltpu.VMEM((ROUNDS, shards, right_rows, LANES), f32),
            pltpu.VMEM((sections * tensors, 8, LANES), f32),
            pltpu.VMEM((rank, max(depth, width)), f32),
            pltpu.SemaphoreType.DMA((ROUNDS, 4, group)),
            pltpu.SemaphoreType.DMA((ROUNDS, 4, shards)),
            pltpu.SemaphoreType.DMA((2, sections * tensors)),
        ],
        compiler_params=pltpu.CompilerParams(
            collective_id=0, has_side_effects=True, vmem_limit_bytes=40 * 2**20
        ),
        cost_estimate=pl.CostEstimate(flops=10**9, bytes_accessed=120 * 10**6, transcendentals=0),
        name="power_rounds",
    )(corrected, factors, whiten)


def update_kernel(
    entries,
    corrected_ref,
    left_ref,
    right_ref,
    total_ref,
    base_ref,
    momentum_ref,
    master_ref,
    errors_out,
    factors_out,
    momentum_out,
    master_out,
    weights_out,
):
    block = pl.program_id(0)
    right = right_ref[...]
    high, low = split(right)
    stacked = jnp.concatenate([high, high, low], axis=0)
    approx = jnp.dot(left_ref[...], stacked, preferred_element_type=f32)
    errors_out[...] = corrected_ref[...] - approx
    spread = jnp.sqrt(total_ref[0:1, 0:1] / entries + epsilon)
    clip = jnp.minimum(1.0, clip_level / spread)
    clipped = clip * approx

    @pl.when(block == 0)
    def _():
        factors_out[...] = right

    own = block == lax.axis_index("shard")

    @pl.when(own)
    def _():
        moved = momentum_decay * momentum_ref[...] + clipped
        stepped = master_ref[...] - learn_rate * moved
        momentum_out[...] = moved
        master_out[...] = stepped
        weights_out[...] = stepped.astype(bf16)

    @pl.when(jnp.logical_not(own))
    def _():
        weights_out[...] = (base_ref[...].astype(f32) - learn_rate * clipped).astype(bf16)


def run_update(shards, entries, corrected, left, right, total, base, momentum, master):
    depth, width = corrected.shape
    rank = right.shape[0]
    rows = depth // shards
    moving = lambda w: pl.BlockSpec((rows, w), lambda i: (i, 0))
    fixed = lambda shape: pl.BlockSpec(shape, lambda i: (0, 0))
    return pl.pallas_call(
        functools.partial(update_kernel, entries),
        grid=(shards,),
        out_shape=(
            jax.ShapeDtypeStruct((depth, width), f32),
            jax.ShapeDtypeStruct((rank, width), f32),
            jax.ShapeDtypeStruct((rows, width), f32),
            jax.ShapeDtypeStruct((rows, width), f32),
            jax.ShapeDtypeStruct((depth, width), bf16),
        ),
        in_specs=[
            moving(width),
            moving(left.shape[1]),
            fixed(right.shape),
            fixed(total.shape),
            moving(width),
            fixed((rows, width)),
            fixed((rows, width)),
        ],
        out_specs=(
            moving(width),
            fixed((rank, width)),
            fixed((rows, width)),
            fixed((rows, width)),
            moving(width),
        ),
        name="apply_update",
    )(corrected, left, right, total, base, momentum, master)


def table_kernel(ids_ref, rows_ref, table_ref, out_ref):
    count = table_ref.shape[0]
    first = pl.program_id(0) * count
    places = lax.broadcasted_iota(jnp.int32, (count, ids_ref.shape[1]), 0)
    hit = places == (ids_ref[...] - first)
    chosen = jnp.where(hit, 1.0, 0.0).astype(bf16)
    grad = jnp.dot(chosen, rows_ref[...], preferred_element_type=f32)
    out_ref[...] = (table_ref[...].astype(f32) - embed_rate * grad).astype(bf16)


def run_table(ids, rows, table):
    count = 512
    return pl.pallas_call(
        table_kernel,
        grid=(table.shape[0] // count,),
        out_shape=jax.ShapeDtypeStruct(table.shape, bf16),
        in_specs=[
            pl.BlockSpec(ids.shape, lambda i: (0, 0)),
            pl.BlockSpec(rows.shape, lambda i: (0, 0)),
            pl.BlockSpec((count, table.shape[1]), lambda i: (i, 0)),
        ],
        out_specs=pl.BlockSpec((count, table.shape[1]), lambda i: (i, 0)),
        name="table_update",
    )(ids, rows, table)


def solution(mesh):
    shards, tensors, sections = (mesh.shape[a] for a in ("shard", "tensor", "section"))
    sizes = (shards, tensors, sections)

    def on_device(
        hidden_acts, out_grads, errors, factors, whiten, momentum, master, table, touched_ids, touched_grads
    ):
        base_own = (master[0] - (learn_rate * momentum_decay) * momentum[0]).astype(bf16)
        base = lax.all_gather(base_own, "shard", axis=0, tiled=True)
        rows = lax.all_gather(touched_grads, ("shard", "section"), axis=0, tiled=True)
        ids = lax.all_gather(touched_ids, ("shard", "section"), axis=0, tiled=True)
        grad = lax.dot_general(
            out_grads[0], hidden_acts[0], (((0,), (0,)), ((), ())), preferred_element_type=f32
        )
        rounded = lax.optimization_barrier(grad.astype(bf16))
        corrected = rounded.astype(f32) + errors[0, 0]
        left, right, total = run_power(sizes, corrected, factors[0], whiten[0])
        entries = sections * corrected.shape[0] * corrected.shape[1] * tensors
        new_errors, new_factors, new_momentum, new_master, new_weights = run_update(
            shards, entries, corrected, left, right, total, base, momentum[0], master[0]
        )
        first_row = lax.axis_index(("shard", "section")) * table.shape[0]
        new_table = run_table((ids - first_row)[None], rows, table)
        return (
            new_errors[None, None],
            new_factors[None],
            new_momentum[None],
            new_master[None],
            new_weights[None],
            new_table,
        )

    in_specs = (
        P("section", "shard", "tensor"),
        P("section", "shard", None),
        P("section", "shard", None, "tensor"),
        P("section", None, "tensor"),
        P("section", None, None, None),
        P("section", "shard", "tensor"),
        P("section", "shard", "tensor"),
        P(("shard", "section"), "tensor"),
        P(("shard", "section")),
        P(("shard", "section"), "tensor"),
    )
    out_specs = (
        P("section", "shard", None, "tensor"),
        P("section", None, "tensor"),
        P("section", "shard", "tensor"),
        P("section", "shard", "tensor"),
        P("section", None, "tensor"),
        P(("shard", "section"), "tensor"),
    )
    return jax.shard_map(on_device, mesh=mesh, in_specs=in_specs, out_specs=out_specs, check_vma=False)
```

time: 398 us -> 157 us (0.39)
  waiting for transfers between devices: 249 us -> 0.02 us
  Pallas kernels: 0 us -> 66 us
  matrix products: 42.2 us -> 9.17 us
  other arithmetic: 19.3 us -> 6.4 us
  blocking collectives: 65.7 us -> 56.8 us
    psum x4 -> x0, waiting for transfers between devices: 249 us -> none  [the longest x2 176 us: on_device(): left_sum = lax.psum(left_part, ('shard', 'tensor'))]
    pallas_call x0 -> x3, Pallas kernels: none -> 66 us  [the longest x1 50.1 us: run_power(): pl.pallas_call(functools.partial(power_kernel, sizes), out_shape=(jax.Sha...]
    dot_general x9 -> x0, matrix products: 32.9 us -> none  [the longest x2 11.4 us: on_device(): lax.dot_general(right_part, corrected, (((1,), (1,)), ((), ())), precisio...]
    psum x1 -> x0, blocking collectives: 14 us -> none  [on_device(): lax.psum(jnp.sum(gram_left * gram_right), ('tensor', 'section'))]
    scatter-add x1 -> x0, other arithmetic: 8.27 us -> none  [on_device(): table_grad = jnp.zeros((vocab_rows, table_width), jnp.float32).at[target]...]
    convert_element_type x2 -> x1, other arithmetic: 6.73 us -> 2.53 us  [on_device(): (master[0] - learn_rate * momentum_decay * momentum[0]).astype(bf16)]
  transfers between devices with their start and end apart: 5 -> 1, of which waited for: 4 -> 0; matrix products, arithmetic and copies ran while one was open for 4% -> 8% of each run, Pallas kernels for 0% -> 37%
where the time goes in v1:
time: 157 us; the launch traced here: 156 us
  Pallas kernels  66 us (42%)
  blocking collectives  56.8 us (36%)
  between operations  14.1 us (9%)
  matrix products  9.17 us (6%)
  other arithmetic  6.4 us (4%)
  local copies, waits for them, and re-layouts  3.91 us (2%)
    pallas_call x1, Pallas kernels, run_power(): pl.pallas_call(functools.partial(power_kernel, sizes), out_shape=(jax.Sha...  50.1 us
    all_gather x1, blocking collectives, on_device(): lax.all_gather(touched_grads, ('shard', 'section'), axis=0, tiled=True)  34.4 us
    all_gather x1, blocking collectives, on_device(): ids = lax.all_gather(touched_ids, ('shard', 'section'), axis=0, tiled=True)  22.4 us
    dot_general x1, matrix products, on_device(): lax.dot_general(out_grads[0], hidden_acts[0], (((0,), (0,)), ((), ())), p...  9.17 us
    pallas_call x1, Pallas kernels, run_update(): pl.pallas_call(functools.partial(update_kernel, entries), grid=(shards,),...  8.41 us
    pallas_call x1, Pallas kernels, run_table(): pl.pallas_call(table_kernel, grid=(table.shape[0] // count,), out_shape=j...  7.44 us
    unnamed x16, local copies, waits for them, and re-layouts  3.91 us
    add x1, other arithmetic, on_device(): corrected = rounded.astype(f32) + errors[0, 0]  3.28 us
  transfers between devices with their start and end apart: 1, of which 0 were waited for; matrix products, arithmetic and copies ran while one was open for 8% of the time, Pallas kernels for 37%

profile of v1, /device:TPU:0, one launch (start us, length us, event | category | flops | bytes accessed | tf_op | source)
XLA Modules:
  0.0 156.4 jit_solution(10524494617223891212)
XLA Ops:
  7.2 0.0 all-gather.3.cloned.1.call-start
  7.2 2.5 %subtract_convert_fusion = bf16[256,1024]{1,0:T(8,128)(2,1)} fusion(f32[1,256,1024]{2,1,0:T(8,128)} %param.15, f32[1,256,1024]{2,1,0:T(8,128)} %param.16), kind=kLoop, calls=%fused_computation.5 | loop fusion | flops 786432 | bytes 2621440 | tf_op jit(solution)/shard_map/convert_element_type | solution.py:364
  9.7 0.0 all-gather.3.cloned.1.call-update
  9.8 0.0 copy-start.7
  9.8 0.0 copy-start.6
  9.8 9.2 %fusion.3 = bf16[1024,1024]{1,0:T(8,128)(2,1)S(1)} fusion(bf16[1,2560,1024]{2,1,0:T(8,128)(2,1)} %param.10, bf16[1,2560,1024]{2,1,0:T(8,128)(2,1)} %param.11), kind=kOutput, calls=%fused_computation.4 | convolution fusion | flops 5369757696 | bytes 12582912 | tf_op jit(solution)/shard_map/dot_general | solution.py:368
  19.0 0.0 copy-done.7
  19.0 22.4 %all-gather = s32[8,1,128]{2,1,0:T(1,128)S(1)} all-gather(s32[1,1,128]{2,1,0:T(1,128)S(1)} %bitcast.30), channel_id=1, replica_groups=mesh['shard'=4,'tensor'=4,'section'=2] {'shard','section'}, dimensions={0}, use_global_device_ids=true | all-gather | bytes 4608 | tf_op jit(solution)/shard_map/all_gather | solution.py:367
  41.4 0.6 subtract_bitcast_fusion.ids_ref
  42.0 0.0 copy-done.6
  42.0 34.4 %all_gather.11.rows_ref = bf16[1024,256]{1,0:T(8,128)(2,1)} all-gather(bf16[128,256]{1,0:T(8,128)(2,1)S(1)} %copy-done.6), channel_id=1, replica_groups=mesh['shard'=4,'tensor'=4,'section'=2] {'shard','section'}, dimensions={0}, use_global_device_ids=true | all-gather | bytes 589824 | tf_op jit(solution)/shard_map/all_gather | solution.py:366
  76.4 7.4 %table_update.1 = bf16[4096,256]{1,0:T(8,128)(2,1)} custom-call(s32[1,1024]{1,0:T(1,128)} %subtract_bitcast_fusion.ids_ref, bf16[1024,256]{1,0:T(8,128)(2,1)} %all_gather.11.rows_ref, bf16[4096,256]{1,0:T(8,128)(2,1)} %table_ref.1), custom_call_target="tpu_custom_call" | custom-call | tf_op jit(solution)/shard_map/table_update/pallas_call | solution.py:343
  83.8 0.0 copy-start.3
  83.9 0.0 copy-start.4
  83.9 3.3 %bitcast_add_fusion.corrected_ref = f32[1024,1024]{1,0:T(8,128)S(1)} fusion(f32[1,1,1024,1024]{3,2,1,0:T(8,128)} %param.12, bf16[1024,1024]{1,0:T(8,128)(2,1)S(1)} %fusion.3), kind=kLoop, calls=%fused_computation.3 | loop fusion | flops 2097152 | bytes 10485760 | tf_op jit(solution)/shard_map/add | solution.py:372
  87.1 0.0 copy-done.3
  87.1 0.0 copy-done.4
  87.2 50.1 %power_rounds.1 = (bf16[1024,96]{1,0:T(8,128)(2,1)S(1)}, f32[32,1024]{1,0:T(8,128)S(1)}, f32[8,128]{1,0:T(8,128)S(1)}) custom-call(f32[1024,1024]{1,0:T(8,128)S(1)} %bitcast_add_fusion.corrected_ref, f32[32,1024]{1,0:T(8,128)S(1)} %bitcast.26, f32[2,32,32]{2,1,0:T(8,128)S(1)} %bitcast.27), custom_call_target="tpu_custom_call" | custom-call | flops 1000000000 | bytes 120000000 | tf_op jit(solution)/shard_map/power_rounds/pallas_call | solution.py:219
  137.3 0.0 copy-start
  137.3 1.9 %copy-done = f32[1024,1024]{1,0:T(8,128)} copy-done((f32[1024,1024]{1,0:T(8,128)}, f32[1024,1024]{1,0:T(8,128)S(1)}, u32[]{:S(2)}) %copy-start) | copy-done | bytes 4194328
  139.2 0.7 copy-done.1
  139.9 0.6 copy-done.2
  140.6 0.6 copy-done.5
  141.2 8.4 %apply_update.1 = (f32[1024,1024]{1,0:T(8,128)}, f32[32,1024]{1,0:T(8,128)}, f32[256,1024]{1,0:T(8,128)}, f32[256,1024]{1,0:T(8,128)}, bf16[1024,1024]{1,0:T(8,128)(2,1)}) custom-call(f32[1024,1024]{1,0:T(8,128)} %copy-done, bf16[1024,96]{1,0:T(8,128)(2,1)} %copy-done.1, f32[32,1024]{1,0:T(8,128)} %copy-done.2, f32[8,128]{1,0:T(8,128)} %copy-done.5, ...), custom_call_target="tpu_custom_call" | custom-call | tf_op jit(solution)/shard_map/apply_update/pallas_call | solution.py:301
  (4 shorter events, 0.0 us)
Async XLA Ops:
  7.2 134.0 %all-gather.3.cloned.1.call-start = ((), (), s32[]{:S(2)}) async-start(), calls=%async_computation | async-start | bytes 2621440 | tf_op jit(solution)/shard_map/all_gather | solution.py:365
  9.8 9.2 %copy-start.7 = (s32[128]{0:T(128)S(1)}, s32[128]{0:T(128)}, u32[]{:S(2)}) copy-start(s32[128]{0:T(128)} %param.18) | copy-start | bytes 1540
  9.8 32.2 %copy-start.6 = (bf16[128,256]{1,0:T(8,128)(2,1)S(1)}, bf16[128,256]{1,0:T(8,128)(2,1)}, u32[]{:S(2)}) copy-start(bf16[128,256]{1,0:T(8,128)(2,1)} %param.19) | copy-start | bytes 196612
  83.8 3.3 %copy-start.3 = (f32[1,32,1024]{2,1,0:T(8,128)S(1)}, f32[1,32,1024]{2,1,0:T(8,128)}, u32[]{:S(2)}) copy-start(f32[1,32,1024]{2,1,0:T(8,128)} %param.13) | copy-start | bytes 393220
  83.9 3.3 %copy-start.4 = (f32[1,2,32,32]{3,2,1,0:T(8,128)S(1)}, f32[1,2,32,32]{3,2,1,0:T(8,128)}, u32[]{:S(2)}) copy-start(f32[1,2,32,32]{3,2,1,0:T(8,128)} %param.14) | copy-start | bytes 24580
  137.3 2.0 %copy-start = (f32[1024,1024]{1,0:T(8,128)}, f32[1024,1024]{1,0:T(8,128)S(1)}, u32[]{:S(2)}) copy-start(f32[1024,1024]{1,0:T(8,128)S(1)} %bitcast_add_fusion.corrected_ref) | copy-start | bytes 12582916
  139.2 0.7 copy-start.1
  139.9 0.7 copy-start.2
  140.6 0.6 copy-start.5
Sparse Core Ops, SparseCore 0:
  10.1 52.6 all-gather.2

commit v2 on v1

--- a/solution.py
+++ b/solution.py
@@ -40,14 +40,44 @@
     return rows, out
 
 
+def pack_rows(ids, touched, vocab, packed):
+    owners, cap, _ = packed.shape
+    count = touched.shape[0]
+    owner = ids // vocab
+    place = ids - owner * vocab
+    owned = lax.broadcasted_iota(jnp.int32, (owners, count), 0) == owner
+    before = lax.broadcasted_iota(jnp.int32, (count, count), 0) < lax.broadcasted_iota(
+        jnp.int32, (count, count), 1
+    )
+    one = lambda mask: jnp.where(mask, 1.0, 0.0)
+    ranks = jnp.dot(one(owned).astype(bf16), one(before).astype(bf16), preferred_element_type=f32)
+    rank = jnp.sum(jnp.where(owned, ranks, 0.0), axis=0, keepdims=True)
+    slot = owner * cap + rank.astype(jnp.int32)
+    chosen = one(lax.broadcasted_iota(jnp.int32, (owners * cap, count), 0) == slot).astype(bf16)
+    line = lax.broadcasted_iota(jnp.int32, (LANES, count), 0)
+    coarse, fine = place // 128, place % 128
+    notes = jnp.where(line == 0, coarse, jnp.where(line == 1, fine, jnp.where(line == 2, 1, 0)))
+    sent = jnp.dot(chosen, touched, preferred_element_type=f32)
+    sent_notes = jnp.dot(chosen, notes.astype(f32).T.astype(bf16), preferred_element_type=f32)
+    width = touched.shape[1]
+    for b in range(owners):
+        packed[b, :, :width] = sent[b * cap : (b + 1) * cap].astype(bf16)
+        packed[b, :, width:] = sent_notes[b * cap : (b + 1) * cap].astype(bf16)
+
+
 def power_kernel(
     sizes,
-    corrected_ref,
+    vocab,
+    grad_ref,
+    errors_ref,
     factors_ref,
     whiten_ref,
+    ids_ref,
+    touched_ref,
     left_ref,
     right_ref,
     total_ref,
+    found_ref,
     high_ref,
     low_ref,
     lsend,
@@ -58,9 +88,12 @@
     rgath,
     square,
     full,
+    packed,
+    found,
     lsem,
     rsem,
     qsem,
+    tsem,
 ):
     shards, tensors, sections = sizes
     rank = factors_ref.shape[0]
@@ -96,10 +129,34 @@
             there = {"section": lax.rem(section + other, sections), "tensor": t}
             pl.semaphore_signal(barrier, inc=1, device_id=there, device_id_type=MESH)
 
-    high, low = split(corrected_ref[...])
+    for other in range(1, sections):
+        for z in range(shards):
+            there = {"section": lax.rem(section + other, sections), "shard": z}
+            pl.semaphore_signal(barrier, inc=1, device_id=there, device_id_type=MESH)
+
+    owners, cap, _ = packed.shape
+    pack_rows(ids_ref[...], touched_ref[...], vocab, packed)
+    block = shard * sections + section
+    pl.semaphore_wait(barrier, group - 1 + (sections - 1) * (tensors + shards))
+
+    def deliver(k):
+        index = lax.rem(block + k, owners)
+        return pltpu.make_async_remote_copy(
+            src_ref=packed.at[index],
+            dst_ref=found.at[block],
+            send_sem=tsem.at[0, k],
+            recv_sem=tsem.at[1, k],
+            device_id={"shard": index // sections, "section": lax.rem(index, sections)},
+            device_id_type=MESH,
+        )
+
+    @pl.loop(1, owners)
+    def _(k):
+        deliver(k).start()
+
+    high, low = split(grad_ref[...].astype(f32) + errors_ref[...])
     high_ref[...] = high
     low_ref[...] = low
-    pl.semaphore_wait(barrier, group - 1 + (sections - 1) * tensors)
 
     def exchange(count, copy):
         @pl.loop(1, count)
@@ -207,24 +264,35 @@
         total = total + square[k]
     total_ref[...] = total
 
-
-def run_power(sizes, corrected, factors, whiten):
+    @pl.loop(1, owners)
+    def _(k):
+        deliver(k).wait()
+
+    found[block] = packed[block]
+    found_ref[...] = found[...]
+
+
+def run_power(sizes, vocab, grad, errors, factors, whiten, ids, touched):
     shards, tensors, sections = sizes
     rank, width = factors.shape
-    depth = corrected.shape[0]
+    depth = grad.shape[0]
+    owners = shards * sections
+    cap = 2 * touched.shape[0] // owners
+    packed = (owners, cap, touched.shape[1] + LANES)
     group = shards * tensors
     left_rows = rank * (depth // LANES) // group
     right_rows = rank * (width // LANES) // shards
     vmem = pl.BlockSpec(memory_space=pltpu.VMEM)
     return pl.pallas_call(
-        functools.partial(power_kernel, sizes),
+        functools.partial(power_kernel, sizes, vocab),
         out_shape=(
             jax.ShapeDtypeStruct((depth, 3 * rank), bf16),
             jax.ShapeDtypeStruct((rank, width), f32),
             jax.ShapeDtypeStruct((8, LANES), f32),
+            jax.ShapeDtypeStruct(packed, bf16),
         ),
-        in_specs=[vmem] * 3,
-        out_specs=(vmem,) * 3,
+        in_specs=[vmem] * 6,
+        out_specs=(vmem,) * 4,
         scratch_shapes=[
             pltpu.VMEM((depth, width), bf16),
             pltpu.VMEM((depth, width), bf16),
@@ -236,21 +304,25 @@
             pltpu.VMEM((ROUNDS, shards, right_rows, LANES), f32),
             pltpu.VMEM((sections * tensors, 8, LANES), f32),
             pltpu.VMEM((rank, max(depth, width)), f32),
+            pltpu.VMEM(packed, bf16),
+            pltpu.VMEM(packed, bf16),
             pltpu.SemaphoreType.DMA((ROUNDS, 4, group)),
             pltpu.SemaphoreType.DMA((ROUNDS, 4, shards)),
             pltpu.SemaphoreType.DMA((2, sections * tensors)),
+            pltpu.SemaphoreType.DMA((2, owners)),
         ],
         compiler_params=pltpu.CompilerParams(
             collective_id=0, has_side_effects=True, vmem_limit_bytes=40 * 2**20
         ),
         cost_estimate=pl.CostEstimate(flops=10**9, bytes_accessed=120 * 10**6, transcendentals=0),
         name="power_rounds",
-    )(corrected, factors, whiten)
+    )(grad, errors, factors, whiten, ids, touched)
 
 
 def update_kernel(
     entries,
-    corrected_ref,
+    grad_ref,
+    errors_ref,
     left_ref,
     right_ref,
     total_ref,
@@ -268,7 +340,7 @@
     high, low = split(right)
     stacked = jnp.concatenate([high, high, low], axis=0)
     approx = jnp.dot(left_ref[...], stacked, preferred_element_type=f32)
-    errors_out[...] = corrected_ref[...] - approx
+    errors_out[...] = (grad_ref[...].astype(f32) + errors_ref[...]) - approx
     spread = jnp.sqrt(total_ref[0:1, 0:1] / entries + epsilon)
     clip = jnp.minimum(1.0, clip_level / spread)
     clipped = clip * approx
@@ -292,8 +364,8 @@
         weights_out[...] = (base_ref[...].astype(f32) - learn_rate * clipped).astype(bf16)
 
 
-def run_update(shards, entries, corrected, left, right, total, base, momentum, master):
-    depth, width = corrected.shape
+def run_update(shards, entries, grad, errors, left, right, total, base, momentum, master):
+    depth, width = errors.shape
     rank = right.shape[0]
     rows = depth // shards
     moving = lambda w: pl.BlockSpec((rows, w), lambda i: (i, 0))
@@ -310,6 +382,7 @@
         ),
         in_specs=[
             moving(width),
+            moving(width),
             moving(left.shape[1]),
             fixed(right.shape),
             fixed(total.shape),
@@ -325,33 +398,34 @@
             moving(width),
         ),
         name="apply_update",
-    )(corrected, left, right, total, base, momentum, master)
-
-
-def table_kernel(ids_ref, rows_ref, table_ref, out_ref):
-    count = table_ref.shape[0]
+    )(grad, errors, left, right, total, base, momentum, master)
+
+
+def table_kernel(found_ref, table_ref, out_ref):
+    count, width = table_ref.shape
     first = pl.program_id(0) * count
-    places = lax.broadcasted_iota(jnp.int32, (count, ids_ref.shape[1]), 0)
-    hit = places == (ids_ref[...] - first)
-    chosen = jnp.where(hit, 1.0, 0.0).astype(bf16)
-    grad = jnp.dot(chosen, rows_ref[...], preferred_element_type=f32)
+    notes = found_ref[:, width:].astype(f32).T
+    place = notes[0:1] * 128.0 + notes[1:2] - (1.0 - notes[2:3])
+    index = place.astype(jnp.int32) - first
+    places = lax.broadcasted_iota(jnp.int32, (count, index.shape[1]), 0)
+    chosen = jnp.where(places == index, 1.0, 0.0).astype(bf16)
+    grad = jnp.dot(chosen, found_ref[:, :width], preferred_element_type=f32)
     out_ref[...] = (table_ref[...].astype(f32) - embed_rate * grad).astype(bf16)
 
 
-def run_table(ids, rows, table):
-    count = 512
+def run_table(found, table):
+    count = 1024
     return pl.pallas_call(
         table_kernel,
         grid=(table.shape[0] // count,),
         out_shape=jax.ShapeDtypeStruct(table.shape, bf16),
         in_specs=[
-            pl.BlockSpec(ids.shape, lambda i: (0, 0)),
-            pl.BlockSpec(rows.shape, lambda i: (0, 0)),
+            pl.BlockSpec(found.shape, lambda i: (0, 0)),
             pl.BlockSpec((count, table.shape[1]), lambda i: (i, 0)),
         ],
         out_specs=pl.BlockSpec((count, table.shape[1]), lambda i: (i, 0)),
         name="table_update",
-    )(ids, rows, table)
+    )(found, table)
 
 
 def solution(mesh):
@@ -363,20 +437,18 @@
     ):
         base_own = (master[0] - (learn_rate * momentum_decay) * momentum[0]).astype(bf16)
         base = lax.all_gather(base_own, "shard", axis=0, tiled=True)
-        rows = lax.all_gather(touched_grads, ("shard", "section"), axis=0, tiled=True)
-        ids = lax.all_gather(touched_ids, ("shard", "section"), axis=0, tiled=True)
         grad = lax.dot_general(
             out_grads[0], hidden_acts[0], (((0,), (0,)), ((), ())), preferred_element_type=f32
         )
-        rounded = lax.optimization_barrier(grad.astype(bf16))
-        corrected = rounded.astype(f32) + errors[0, 0]
-        left, right, total = run_power(sizes, corrected, factors[0], whiten[0])
-        entries = sections * corrected.shape[0] * corrected.shape[1] * tensors
+        rounded = grad.astype(bf16)
+        left, right, total, found = run_power(
+            sizes, table.shape[0], rounded, errors[0, 0], factors[0], whiten[0], touched_ids[None], touched_grads
+        )
+        entries = sections * rounded.shape[0] * rounded.shape[1] * tensors
         new_errors, new_factors, new_momentum, new_master, new_weights = run_update(
-            shards, entries, corrected, left, right, total, base, momentum[0], master[0]
-        )
-        first_row = lax.axis_index(("shard", "section")) * table.shape[0]
-        new_table = run_table((ids - first_row)[None], rows, table)
+            shards, entries, rounded, errors[0, 0], left, right, total, base, momentum[0], master[0]
+        )
+        new_table = run_table(found.reshape(-1, found.shape[2]), table)
         return (
             new_errors[None, None],
             new_factors[None],

time: 157 us -> 119 us (0.76)
  blocking collectives: 56.8 us -> 0 us
  Pallas kernels: 66 us -> 89.9 us
  other arithmetic: 6.4 us -> 2.53 us
    all_gather x2 -> x0, blocking collectives: 56.8 us -> none  [the longest x1 34.4 us: on_device(): lax.all_gather(touched_grads, ('shard', 'section'), axis=0, tiled=True)]
    pallas_call x1, Pallas kernels: 50.1 us -> 76.5 us  [run_power(): pl.pallas_call(functools.partial(power_kernel, sizes, vocab), out_shape=(...]
    add x1 -> x0, other arithmetic: 3.28 us -> none  [on_device(): corrected = rounded.astype(f32) + errors[0, 0]]
    pallas_call x1, Pallas kernels: 7.44 us -> 4.44 us  [run_table(): pl.pallas_call(table_kernel, grid=(table.shape[0] // count,), out_shape=j...]
    unnamed x16 -> x20, local copies, waits for them, and re-layouts: 3.91 us -> 2.67 us
  transfers between devices with their start and end apart: 1 -> 1, of which waited for: 0 -> 0; matrix products, arithmetic and copies ran while one was open for 8% -> 8% of each run, Pallas kernels for 37% -> 68%
where the time goes in v2:
time: 119 us
  Pallas kernels  89.9 us (76%)
  between operations  14.1 us (12%)
  matrix products  9.27 us (8%)
  local copies, waits for them, and re-layouts  2.67 us (2%)
  other arithmetic  2.53 us (2%)
    pallas_call x1, Pallas kernels, run_power(): pl.pallas_call(functools.partial(power_kernel, sizes, vocab), out_shape=(...  76.5 us
    dot_general x1, matrix products, on_device(): lax.dot_general(out_grads[0], hidden_acts[0], (((0,), (0,)), ((), ())), p...  9.27 us
    pallas_call x1, Pallas kernels, run_update(): pl.pallas_call(functools.partial(update_kernel, entries), grid=(shards,),...  8.9 us
    pallas_call x1, Pallas kernels, run_table(): pl.pallas_call(table_kernel, grid=(table.shape[0] // count,), out_shape=j...  4.44 us
    unnamed x20, local copies, waits for them, and re-layouts  2.67 us
    convert_element_type x1, other arithmetic, on_device(): (master[0] - learn_rate * momentum_decay * momentum[0]).astype(bf16)  2.53 us
  transfers between devices with their start and end apart: 1, of which 0 were waited for; matrix products, arithmetic and copies ran while one was open for 8% of the time, Pallas kernels for 68%

profile of v2, /device:TPU:0, one launch (start us, length us, event | category | flops | bytes accessed | tf_op | source)
XLA Modules:
  0.0 118.5 jit_solution(16297941317989721182)
XLA Ops:
  7.2 0.0 all-gather.2.cloned.1.call-start
  7.2 2.5 %subtract_convert_fusion = bf16[256,1024]{1,0:T(8,128)(2,1)} fusion(f32[1,256,1024]{2,1,0:T(8,128)} %param.15, f32[1,256,1024]{2,1,0:T(8,128)} %param.16), kind=kLoop, calls=%fused_computation.4 | loop fusion | flops 786432 | bytes 2621440 | tf_op jit(solution)/shard_map/convert_element_type | solution.py:438
  9.7 0.0 all-gather.2.cloned.1.call-update
  9.8 0.0 copy-start
  9.8 0.0 copy-start.5
  9.8 0.0 copy-start.6
  9.8 0.0 copy-start.7
  9.8 0.0 copy-start.9
  9.8 9.3 %fusion.3.grad_ref = bf16[1024,1024]{1,0:T(8,128)(2,1)S(1)} fusion(bf16[1,2560,1024]{2,1,0:T(8,128)(2,1)} %param.10, bf16[1,2560,1024]{2,1,0:T(8,128)(2,1)} %param.11), kind=kOutput, calls=%fused_computation.3 | convolution fusion | flops 5369757696 | bytes 12582912 | tf_op jit(solution)/shard_map/dot_general | solution.py:440
  19.1 0.0 copy-start.1
  19.1 0.0 copy-done
  19.1 0.0 copy-done.5
  19.1 0.0 copy-done.6
  19.2 0.0 copy-done.7
  19.2 0.0 copy-done.9
  19.2 76.5 %power_rounds.1 = (bf16[1024,96]{1,0:T(8,128)(2,1)S(1)}, f32[32,1024]{1,0:T(8,128)S(1)}, f32[8,128]{1,0:T(8,128)S(1)}, bf16[8,32,384]{2,1,0:T(8,128)(2,1)S(1)}) custom-call(bf16[1024,1024]{1,0:T(8,128)(2,1)S(1)} %fusion.3.grad_ref, f32[1024,1024]{1,0:T(8,128)S(1)} %bitcast.25, f32[32,1024]{1,0:T(8,128)S(1)} %bitcast.27, f32[2,32,32]{2,1,0:T(8,128)S(1)} %bitcast.28, ...), custom_call_target="tpu_custom_call" | custom-call | flops 1000000000 | bytes 120000000 | tf_op jit(solution)/shard_map/power_rounds/pallas_call | solution.py:286
  95.7 0.0 copy-start.2
  95.7 0.7 copy-done.2
  96.4 0.7 copy-done.3
  97.1 0.7 copy-done.4
  97.8 0.6 copy-done.8
  98.3 4.4 %table_update.1 = bf16[4096,256]{1,0:T(8,128)(2,1)} custom-call(bf16[256,384]{1,0:T(8,128)(2,1)} %bitcast.26, bf16[4096,256]{1,0:T(8,128)(2,1)} %table_ref.1), custom_call_target="tpu_custom_call" | custom-call | tf_op jit(solution)/shard_map/table_update/pallas_call | solution.py:418
  102.8 0.0 copy-done.1
  102.8 8.9 %apply_update.1 = (f32[1024,1024]{1,0:T(8,128)}, f32[32,1024]{1,0:T(8,128)}, f32[256,1024]{1,0:T(8,128)}, f32[256,1024]{1,0:T(8,128)}, bf16[1024,1024]{1,0:T(8,128)(2,1)}) custom-call(bf16[1024,1024]{1,0:T(8,128)(2,1)} %copy-done.1, f32[1024,1024]{1,0:T(8,128)} %bitcast.24, bf16[1024,96]{1,0:T(8,128)(2,1)} %copy-done.2, f32[32,1024]{1,0:T(8,128)} %copy-done.4, ...), custom_call_target="tpu_custom_call" | custom-call | tf_op jit(solution)/shard_map/apply_update/pallas_call | solution.py:373
  (4 shorter events, 0.0 us)
Async XLA Ops:
  7.2 95.6 %all-gather.2.cloned.1.call-start = ((), (), s32[]{:S(2)}) async-start(), calls=%async_computation | async-start | bytes 2621440 | tf_op jit(solution)/shard_map/all_gather | solution.py:439
  9.8 9.4 %copy-start = (f32[1,1,1024,1024]{3,2,1,0:T(8,128)S(1)}, f32[1,1,1024,1024]{3,2,1,0:T(8,128)}, u32[]{:S(2)}) copy-start(f32[1,1,1024,1024]{3,2,1,0:T(8,128)} %param.12) | copy-start | bytes 12582916
  9.8 9.4 %copy-start.5 = (f32[1,32,1024]{2,1,0:T(8,128)S(1)}, f32[1,32,1024]{2,1,0:T(8,128)}, u32[]{:S(2)}) copy-start(f32[1,32,1024]{2,1,0:T(8,128)} %param.13) | copy-start | bytes 393220
  9.8 9.4 %copy-start.6 = (bf16[128,256]{1,0:T(8,128)(2,1)S(1)}, bf16[128,256]{1,0:T(8,128)(2,1)}, u32[]{:S(2)}) copy-start(bf16[128,256]{1,0:T(8,128)(2,1)} %touched_ref.1) | copy-start | bytes 196612
  9.8 9.3 %copy-start.7 = (f32[1,2,32,32]{3,2,1,0:T(8,128)S(1)}, f32[1,2,32,32]{3,2,1,0:T(8,128)}, u32[]{:S(2)}) copy-start(f32[1,2,32,32]{3,2,1,0:T(8,128)} %param.14) | copy-start | bytes 24580
  9.8 9.3 %copy-start.9 = (s32[128]{0:T(128)S(1)}, s32[128]{0:T(128)}, u32[]{:S(2)}) copy-start(s32[128]{0:T(128)} %param.18) | copy-start | bytes 1540
  19.1 83.7 %copy-start.1 = (bf16[1024,1024]{1,0:T(8,128)(2,1)}, bf16[1024,1024]{1,0:T(8,128)(2,1)S(1)}, u32[]{:S(2)}) copy-start(bf16[1024,1024]{1,0:T(8,128)(2,1)S(1)} %fusion.3.grad_ref) | copy-start | bytes 6291460
  95.7 0.7 copy-start.2
  96.4 0.7 copy-start.3
  97.1 0.7 copy-start.4
  97.7 0.6 copy-start.8
Sparse Core Ops, SparseCore 0:
  10.1 66.7 all-gather.1

commit v3 on v2

--- a/solution.py
+++ b/solution.py
@@ -74,10 +74,13 @@
     whiten_ref,
     ids_ref,
     touched_ref,
+    momentum_ref,
+    master_ref,
     left_ref,
     right_ref,
     total_ref,
     found_ref,
+    base_ref,
     high_ref,
     low_ref,
     lsend,
@@ -93,7 +96,9 @@
     lsem,
     rsem,
     qsem,
+    base_own,
     tsem,
+    bsem,
 ):
     shards, tensors, sections = sizes
     rank = factors_ref.shape[0]
@@ -134,6 +139,7 @@
             there = {"section": lax.rem(section + other, sections), "shard": z}
             pl.semaphore_signal(barrier, inc=1, device_id=there, device_id_type=MESH)
 
+    base_own[...] = (master_ref[...] - (learn_rate * momentum_decay) * momentum_ref[...]).astype(bf16)
     owners, cap, _ = packed.shape
     pack_rows(ids_ref[...], touched_ref[...], vocab, packed)
     block = shard * sections + section
@@ -154,6 +160,40 @@
     def _(k):
         deliver(k).start()
 
+    def carry(way, step, receiving=False):
+        sign = 1 if way == 0 else -1
+        at = shard - sign if receiving else shard
+        index = lax.rem(at - sign * step + 2 * shards, shards)
+        return pltpu.make_async_remote_copy(
+            src_ref=base_own if step == 0 and not receiving else base_ref.at[index],
+            dst_ref=base_ref.at[index],
+            send_sem=bsem.at[way, 0, step],
+            recv_sem=bsem.at[way, 1, step],
+            device_id={"shard": lax.rem(shard + sign + shards, shards)},
+            device_id_type=MESH,
+        )
+
+    def sends(way, step):
+        if way == 0:
+            return jnp.logical_and(shard >= step, shard < shards - 1)
+        return jnp.logical_and(shard < shards - step, shard > 0)
+
+    def advance(step):
+        for way in (0, 1):
+            if step > 0:
+                arrives = shard >= step if way == 0 else shard < shards - step
+
+                @pl.when(arrives)
+                def _():
+                    carry(way, step - 1, True).wait_recv()
+
+            if step < shards - 1:
+
+                @pl.when(sends(way, step))
+                def _():
+                    carry(way, step).start()
+
+    advance(0)
     high, low = split(grad_ref[...].astype(f32) + errors_ref[...])
     high_ref[...] = high
     low_ref[...] = low
@@ -217,6 +257,8 @@
     right = factors_ref[...]
     left_unit = None
     for turn in range(ROUNDS):
+        if 0 < 2 * turn < shards - 1:
+            advance(2 * turn)
         left_part = times(right, ((1,), (1,)))
         left = all_reduce(
             left_part, group, me, left_peer, lsend.at[turn], lrecv.at[turn], lgath.at[turn], lsem.at[turn]
@@ -225,6 +267,8 @@
             whiten_ref[turn], left, (((0,), (0,)), ((), ())), precision=highest, preferred_element_type=f32
         )
         left_unit = whitened * lax.rsqrt(jnp.sum(whitened * whitened) / rank + epsilon)
+        if 2 * turn + 1 < shards - 1:
+            advance(2 * turn + 1)
         right_part = times(left_unit, ((1,), (0,)))
         right = all_reduce(
             right_part, shards, shard, right_peer, rsend.at[turn], rrecv.at[turn], rgath.at[turn], rsem.at[turn]
@@ -268,11 +312,20 @@
     def _(k):
         deliver(k).wait()
 
+    for step in range(min(2 * ROUNDS, shards - 1), shards):
+        advance(step)
+    for step in range(shards - 1):
+        for way in (0, 1):
+
+            @pl.when(sends(way, step))
+            def _():
+                carry(way, step).wait_send()
+
     found[block] = packed[block]
     found_ref[...] = found[...]
 
 
-def run_power(sizes, vocab, grad, errors, factors, whiten, ids, touched):
+def run_power(sizes, vocab, grad, errors, factors, whiten, ids, touched, momentum, master):
     shards, tensors, sections = sizes
     rank, width = factors.shape
     depth = grad.shape[0]
@@ -290,9 +343,10 @@
             jax.ShapeDtypeStruct((rank, width), f32),
             jax.ShapeDtypeStruct((8, LANES), f32),
             jax.ShapeDtypeStruct(packed, bf16),
+            jax.ShapeDtypeStruct((shards,) + master.shape, bf16),
         ),
-        in_specs=[vmem] * 6,
-        out_specs=(vmem,) * 4,
+        in_specs=[vmem] * 8,
+        out_specs=(vmem,) * 4 + (pl.BlockSpec(memory_space=pl.ANY),),
         scratch_shapes=[
             pltpu.VMEM((depth, width), bf16),
             pltpu.VMEM((depth, width), bf16),
@@ -309,14 +363,16 @@
             pltpu.SemaphoreType.DMA((ROUNDS, 4, group)),
             pltpu.SemaphoreType.DMA((ROUNDS, 4, shards)),
             pltpu.SemaphoreType.DMA((2, sections * tensors)),
+            pltpu.VMEM(master.shape, bf16),
             pltpu.SemaphoreType.DMA((2, owners)),
+            pltpu.SemaphoreType.DMA((2, 2, shards)),
         ],
         compiler_params=pltpu.CompilerParams(
             collective_id=0, has_side_effects=True, vmem_limit_bytes=40 * 2**20
         ),
         cost_estimate=pl.CostEstimate(flops=10**9, bytes_accessed=120 * 10**6, transcendentals=0),
         name="power_rounds",
-    )(grad, errors, factors, whiten, ids, touched)
+    )(grad, errors, factors, whiten, ids, touched, momentum, master)
 
 
 def update_kernel(
@@ -349,14 +405,17 @@
     def _():
         factors_out[...] = right
 
-    own = block == lax.axis_index("shard")
+    rows = approx.shape[0]
+    parts = momentum_ref.shape[0] // rows
+    own = block // parts == lax.axis_index("shard")
+    here = pl.ds(pl.multiple_of(lax.rem(block, parts) * rows, rows), rows)
 
     @pl.when(own)
     def _():
-        moved = momentum_decay * momentum_ref[...] + clipped
-        stepped = master_ref[...] - learn_rate * moved
-        momentum_out[...] = moved
-        master_out[...] = stepped
+        moved = momentum_decay * momentum_ref[here, :] + clipped
+        stepped = master_ref[here, :] - learn_rate * moved
+        momentum_out[here, :] = moved
+        master_out[here, :] = stepped
         weights_out[...] = stepped.astype(bf16)
 
     @pl.when(jnp.logical_not(own))
@@ -368,11 +427,12 @@
     depth, width = errors.shape
     rank = right.shape[0]
     rows = depth // shards
-    moving = lambda w: pl.BlockSpec((rows, w), lambda i: (i, 0))
+    parts = 2
+    moving = lambda w: pl.BlockSpec((rows // parts, w), lambda i: (i, 0))
     fixed = lambda shape: pl.BlockSpec(shape, lambda i: (0, 0))
     return pl.pallas_call(
         functools.partial(update_kernel, entries),
-        grid=(shards,),
+        grid=(shards * parts,),
         out_shape=(
             jax.ShapeDtypeStruct((depth, width), f32),
             jax.ShapeDtypeStruct((rank, width), f32),
@@ -435,18 +495,17 @@
     def on_device(
         hidden_acts, out_grads, errors, factors, whiten, momentum, master, table, touched_ids, touched_grads
     ):
-        base_own = (master[0] - (learn_rate * momentum_decay) * momentum[0]).astype(bf16)
-        base = lax.all_gather(base_own, "shard", axis=0, tiled=True)
         grad = lax.dot_general(
             out_grads[0], hidden_acts[0], (((0,), (0,)), ((), ())), preferred_element_type=f32
         )
         rounded = grad.astype(bf16)
-        left, right, total, found = run_power(
-            sizes, table.shape[0], rounded, errors[0, 0], factors[0], whiten[0], touched_ids[None], touched_grads
+        left, right, total, found, base = run_power(
+            sizes, table.shape[0], rounded, errors[0, 0], factors[0], whiten[0], touched_ids[None], touched_grads,
+            momentum[0], master[0],
         )
         entries = sections * rounded.shape[0] * rounded.shape[1] * tensors
         new_errors, new_factors, new_momentum, new_master, new_weights = run_update(
-            shards, entries, rounded, errors[0, 0], left, right, total, base, momentum[0], master[0]
+            shards, entries, rounded, errors[0, 0], left, right, total, base.reshape(rounded.shape), momentum[0], master[0]
         )
         new_table = run_table(found.reshape(-1, found.shape[2]), table)
         return (

time: 119 us -> 117 us (0.983)
  between operations: 14.1 us -> 0.79 us
  Pallas kernels: 89.9 us -> 103 us
  other arithmetic: 2.53 us -> 0 us
  local copies, waits for them, and re-layouts: 2.67 us -> 3.99 us
    pallas_call x1, Pallas kernels: 76.5 us -> 87.5 us  [run_power(): pl.pallas_call(functools.partial(power_kernel, sizes, vocab), out_shape=(...]
    convert_element_type x1 -> x0, other arithmetic: 2.53 us -> none  [on_device(): (master[0] - learn_rate * momentum_decay * momentum[0]).astype(bf16)]
    pallas_call x1, Pallas kernels: 8.9 us -> 10.8 us  [run_update(): pl.pallas_call(functools.partial(update_kernel, entries), grid=(shards *...]
    unnamed x20 -> x26, local copies, waits for them, and re-layouts: 2.67 us -> 3.99 us
  transfers between devices with their start and end apart: 1 -> 0, of which waited for: 0 -> 0; matrix products, arithmetic and copies ran while one was open for 8% -> 0% of each run, Pallas kernels for 68% -> 0%
where the time goes in v3:
time: 117 us
  Pallas kernels  103 us (88%)
  matrix products  9.28 us (8%)
  local copies, waits for them, and re-layouts  3.99 us (3%)
    pallas_call x1, Pallas kernels, run_power(): pl.pallas_call(functools.partial(power_kernel, sizes, vocab), out_shape=(...  87.5 us
    pallas_call x1, Pallas kernels, run_update(): pl.pallas_call(functools.partial(update_kernel, entries), grid=(shards *...  10.8 us
    dot_general x1, matrix products, on_device(): lax.dot_general(out_grads[0], hidden_acts[0], (((0,), (0,)), ((), ())), p...  9.28 us
    pallas_call x1, Pallas kernels, run_table(): pl.pallas_call(table_kernel, grid=(table.shape[0] // count,), out_shape=j...  4.45 us
    unnamed x26, local copies, waits for them, and re-layouts  3.99 us

profile of v3, /device:TPU:0, one launch (start us, length us, event | category | flops | bytes accessed | tf_op | source)
XLA Modules:
  0.0 116.7 jit_solution(496806227625030765)
XLA Ops:
  0.6 0.0 copy-start
  0.6 0.0 copy-start.2
  0.7 0.0 copy-start.3
  0.7 0.0 copy-start.7
  0.7 0.0 copy-start.10
  0.7 0.0 copy-start.12
  0.7 0.0 copy-start.9
  0.7 9.3 %fusion.3.grad_ref = bf16[1024,1024]{1,0:T(8,128)(2,1)S(1)} fusion(bf16[1,2560,1024]{2,1,0:T(8,128)(2,1)} %param.10, bf16[1,2560,1024]{2,1,0:T(8,128)(2,1)} %param.11), kind=kOutput, calls=%fused_computation.3 | convolution fusion | flops 5369757696 | bytes 12582912 | tf_op jit(solution)/shard_map/dot_general | solution.py:498
  10.0 0.0 copy-start.1
  10.0 0.0 copy-done
  10.0 0.0 copy-done.2
  10.0 0.0 copy-done.3
  10.0 0.0 copy-done.7
  10.0 0.0 copy-done.10
  10.1 0.0 copy-done.12
  10.1 0.0 copy-done.9
  10.1 87.5 %power_rounds.1 = (bf16[1024,96]{1,0:T(8,128)(2,1)S(1)}, f32[32,1024]{1,0:T(8,128)S(1)}, f32[8,128]{1,0:T(8,128)S(1)}, bf16[8,32,384]{2,1,0:T(8,128)(2,1)S(1)}, bf16[4,256,1024]{2,1,0:T(8,128)(2,1)S(1)}) custom-call(bf16[1024,1024]{1,0:T(8,128)(2,1)S(1)} %fusion.3.grad_ref, f32[1024,1024]{1,0:T(8,128)S(1)} %bitcast.24, f32[32,1024]{1,0:T(8,128)S(1)} %bitcast.31, ...), custom_call_target="tpu_custom_call" | custom-call | flops 1000000000 | bytes 120000000 | tf_op jit(solution)/shard_map/power_rounds/pallas_call | solution.py:339
  97.6 1.3 %copy-done.4 = bf16[4,256,1024]{2,1,0:T(8,128)(2,1)} copy-done((bf16[4,256,1024]{2,1,0:T(8,128)(2,1)}, bf16[4,256,1024]{2,1,0:T(8,128)(2,1)S(1)}, u32[]{:S(2)}) %copy-start.4) | copy-done | bytes 2097176
  98.9 0.7 copy-done.5
  99.6 0.7 copy-done.6
  100.3 0.7 copy-done.8
  100.9 0.6 copy-done.11
  101.5 10.8 %apply_update.1 = (f32[1024,1024]{1,0:T(8,128)}, f32[32,1024]{1,0:T(8,128)}, f32[256,1024]{1,0:T(8,128)}, f32[256,1024]{1,0:T(8,128)}, bf16[1024,1024]{1,0:T(8,128)(2,1)}) custom-call(bf16[1024,1024]{1,0:T(8,128)(2,1)} %copy-done.1, f32[1024,1024]{1,0:T(8,128)} %bitcast.23, bf16[1024,96]{1,0:T(8,128)(2,1)} %copy-done.5, f32[32,1024]{1,0:T(8,128)} %copy-done.8, ...), custom_call_target="tpu_custom_call" | custom-call | tf_op jit(solution)/shard_map/apply_update/pallas_call | solution.py:433
  112.3 4.4 %table_update.1 = bf16[4096,256]{1,0:T(8,128)(2,1)} custom-call(bf16[256,384]{1,0:T(8,128)(2,1)} %bitcast.30, bf16[4096,256]{1,0:T(8,128)(2,1)} %table_ref.1), custom_call_target="tpu_custom_call" | custom-call | tf_op jit(solution)/shard_map/table_update/pallas_call | solution.py:478
  (6 shorter events, 0.0 us)
Async XLA Ops:
  0.6 9.4 %copy-start = (f32[1,1,1024,1024]{3,2,1,0:T(8,128)S(1)}, f32[1,1,1024,1024]{3,2,1,0:T(8,128)}, u32[]{:S(2)}) copy-start(f32[1,1,1024,1024]{3,2,1,0:T(8,128)} %param.12) | copy-start | bytes 12582916
  0.6 9.4 %copy-start.2 = (f32[1,256,1024]{2,1,0:T(8,128)S(1)}, f32[1,256,1024]{2,1,0:T(8,128)}, u32[]{:S(2)}) copy-start(f32[1,256,1024]{2,1,0:T(8,128)} %param.15) | copy-start | bytes 3145732
  0.7 9.4 %copy-start.3 = (f32[1,256,1024]{2,1,0:T(8,128)S(1)}, f32[1,256,1024]{2,1,0:T(8,128)}, u32[]{:S(2)}) copy-start(f32[1,256,1024]{2,1,0:T(8,128)} %param.16) | copy-start | bytes 3145732
  0.7 9.4 %copy-start.7 = (f32[1,32,1024]{2,1,0:T(8,128)S(1)}, f32[1,32,1024]{2,1,0:T(8,128)}, u32[]{:S(2)}) copy-start(f32[1,32,1024]{2,1,0:T(8,128)} %param.13) | copy-start | bytes 393220
  0.7 9.4 %copy-start.10 = (f32[1,2,32,32]{3,2,1,0:T(8,128)S(1)}, f32[1,2,32,32]{3,2,1,0:T(8,128)}, u32[]{:S(2)}) copy-start(f32[1,2,32,32]{3,2,1,0:T(8,128)} %param.14) | copy-start | bytes 24580
  0.7 9.4 %copy-start.12 = (s32[128]{0:T(128)S(1)}, s32[128]{0:T(128)}, u32[]{:S(2)}) copy-start(s32[128]{0:T(128)} %param.18) | copy-start | bytes 1540
  0.7 9.4 %copy-start.9 = (bf16[128,256]{1,0:T(8,128)(2,1)S(1)}, bf16[128,256]{1,0:T(8,128)(2,1)}, u32[]{:S(2)}) copy-start(bf16[128,256]{1,0:T(8,128)(2,1)} %touched_ref.1) | copy-start | bytes 196612
  10.0 87.5 %copy-start.1 = (bf16[1024,1024]{1,0:T(8,128)(2,1)}, bf16[1024,1024]{1,0:T(8,128)(2,1)S(1)}, u32[]{:S(2)}) copy-start(bf16[1024,1024]{1,0:T(8,128)(2,1)S(1)} %fusion.3.grad_ref) | copy-start | bytes 6291460
  97.5 1.3 %copy-start.4 = (bf16[4,256,1024]{2,1,0:T(8,128)(2,1)}, bf16[4,256,1024]{2,1,0:T(8,128)(2,1)S(1)}, u32[]{:S(2)}) copy-start(bf16[4,256,1024]{2,1,0:T(8,128)(2,1)S(1)} %get-tuple-element.19) | copy-start | bytes 6291460
  98.9 0.7 copy-start.5
  99.6 0.7 copy-start.6
  100.3 0.7 copy-start.8
  100.9 0.6 copy-start.11

commit v4 on v3

--- a/solution.py
+++ b/solution.py
@@ -74,8 +74,8 @@
     whiten_ref,
     ids_ref,
     touched_ref,
-    momentum_ref,
-    master_ref,
+    below_ref,
+    above_ref,
     left_ref,
     right_ref,
     total_ref,
@@ -96,9 +96,9 @@
     lsem,
     rsem,
     qsem,
-    base_own,
     tsem,
     bsem,
+    nsem,
 ):
     shards, tensors, sections = sizes
     rank = factors_ref.shape[0]
@@ -139,7 +139,6 @@
             there = {"section": lax.rem(section + other, sections), "shard": z}
             pl.semaphore_signal(barrier, inc=1, device_id=there, device_id_type=MESH)
 
-    base_own[...] = (master_ref[...] - (learn_rate * momentum_decay) * momentum_ref[...]).astype(bf16)
     owners, cap, _ = packed.shape
     pack_rows(ids_ref[...], touched_ref[...], vocab, packed)
     block = shard * sections + section
@@ -160,12 +159,25 @@
     def _(k):
         deliver(k).start()
 
+    near = (below_ref, above_ref)
+
+    def keep(way):
+        index = lax.rem(shard + (shards - 1 if way == 0 else 1), shards)
+        return pltpu.make_async_copy(near[way], base_ref.at[index], nsem.at[way])
+
+    holds = (shard > 0, shard < shards - 1)
+    for way in (0, 1):
+
+        @pl.when(holds[way])
+        def _():
+            keep(way).start()
+
     def carry(way, step, receiving=False):
         sign = 1 if way == 0 else -1
         at = shard - sign if receiving else shard
         index = lax.rem(at - sign * step + 2 * shards, shards)
         return pltpu.make_async_remote_copy(
-            src_ref=base_own if step == 0 and not receiving else base_ref.at[index],
+            src_ref=near[way] if step == 1 and not receiving else base_ref.at[index],
             dst_ref=base_ref.at[index],
             send_sem=bsem.at[way, 0, step],
             recv_sem=bsem.at[way, 1, step],
@@ -180,7 +192,7 @@
 
     def advance(step):
         for way in (0, 1):
-            if step > 0:
+            if step > 1:
                 arrives = shard >= step if way == 0 else shard < shards - step
 
                 @pl.when(arrives)
@@ -193,7 +205,7 @@
                 def _():
                     carry(way, step).start()
 
-    advance(0)
+    advance(1)
     high, low = split(grad_ref[...].astype(f32) + errors_ref[...])
     high_ref[...] = high
     low_ref[...] = low
@@ -257,8 +269,8 @@
     right = factors_ref[...]
     left_unit = None
     for turn in range(ROUNDS):
-        if 0 < 2 * turn < shards - 1:
-            advance(2 * turn)
+        if turn == 1 and shards > 3:
+            advance(2)
         left_part = times(right, ((1,), (1,)))
         left = all_reduce(
             left_part, group, me, left_peer, lsend.at[turn], lrecv.at[turn], lgath.at[turn], lsem.at[turn]
@@ -267,8 +279,6 @@
             whiten_ref[turn], left, (((0,), (0,)), ((), ())), precision=highest, preferred_element_type=f32
         )
         left_unit = whitened * lax.rsqrt(jnp.sum(whitened * whitened) / rank + epsilon)
-        if 2 * turn + 1 < shards - 1:
-            advance(2 * turn + 1)
         right_part = times(left_unit, ((1,), (0,)))
         right = all_reduce(
             right_part, shards, shard, right_peer, rsend.at[turn], rrecv.at[turn], rgath.at[turn], rsem.at[turn]
@@ -312,9 +322,15 @@
     def _(k):
         deliver(k).wait()
 
-    for step in range(min(2 * ROUNDS, shards - 1), shards):
+    for step in range(min(3, shards - 1), shards):
         advance(step)
-    for step in range(shards - 1):
+    for way in (0, 1):
+
+        @pl.when(holds[way])
+        def _():
+            keep(way).wait()
+
+    for step in range(1, shards - 1):
         for way in (0, 1):
 
             @pl.when(sends(way, step))
@@ -325,7 +341,7 @@
     found_ref[...] = found[...]
 
 
-def run_power(sizes, vocab, grad, errors, factors, whiten, ids, touched, momentum, master):
+def run_power(sizes, vocab, grad, errors, factors, whiten, ids, touched, below, above):
     shards, tensors, sections = sizes
     rank, width = factors.shape
     depth = grad.shape[0]
@@ -343,7 +359,7 @@
             jax.ShapeDtypeStruct((rank, width), f32),
             jax.ShapeDtypeStruct((8, LANES), f32),
             jax.ShapeDtypeStruct(packed, bf16),
-            jax.ShapeDtypeStruct((shards,) + master.shape, bf16),
+            jax.ShapeDtypeStruct((shards,) + below.shape, bf16),
         ),
         in_specs=[vmem] * 8,
         out_specs=(vmem,) * 4 + (pl.BlockSpec(memory_space=pl.ANY),),
@@ -363,16 +379,16 @@
             pltpu.SemaphoreType.DMA((ROUNDS, 4, group)),
             pltpu.SemaphoreType.DMA((ROUNDS, 4, shards)),
             pltpu.SemaphoreType.DMA((2, sections * tensors)),
-            pltpu.VMEM(master.shape, bf16),
             pltpu.SemaphoreType.DMA((2, owners)),
             pltpu.SemaphoreType.DMA((2, 2, shards)),
+            pltpu.SemaphoreType.DMA((2,)),
         ],
         compiler_params=pltpu.CompilerParams(
             collective_id=0, has_side_effects=True, vmem_limit_bytes=40 * 2**20
         ),
         cost_estimate=pl.CostEstimate(flops=10**9, bytes_accessed=120 * 10**6, transcendentals=0),
         name="power_rounds",
-    )(grad, errors, factors, whiten, ids, touched, momentum, master)
+    )(grad, errors, factors, whiten, ids, touched, below, above)
 
 
 def update_kernel(
@@ -427,7 +443,7 @@
     depth, width = errors.shape
     rank = right.shape[0]
     rows = depth // shards
-    parts = 2
+    parts = 1
     moving = lambda w: pl.BlockSpec((rows // parts, w), lambda i: (i, 0))
     fixed = lambda shape: pl.BlockSpec(shape, lambda i: (0, 0))
     return pl.pallas_call(
@@ -495,13 +511,16 @@
     def on_device(
         hidden_acts, out_grads, errors, factors, whiten, momentum, master, table, touched_ids, touched_grads
     ):
+        base_own = (master[0] - (learn_rate * momentum_decay) * momentum[0]).astype(bf16)
+        below = lax.ppermute(base_own, "shard", [(i, i + 1) for i in range(shards - 1)])
+        above = lax.ppermute(base_own, "shard", [(i + 1, i) for i in range(shards - 1)])
         grad = lax.dot_general(
             out_grads[0], hidden_acts[0], (((0,), (0,)), ((), ())), preferred_element_type=f32
         )
         rounded = grad.astype(bf16)
         left, right, total, found, base = run_power(
             sizes, table.shape[0], rounded, errors[0, 0], factors[0], whiten[0], touched_ids[None], touched_grads,
-            momentum[0], master[0],
+            below, above,
         )
         entries = sections * rounded.shape[0] * rounded.shape[1] * tensors
         new_errors, new_factors, new_momentum, new_master, new_weights = run_update(

time: 117 us -> 115 us (0.983)
  Pallas kernels: 103 us -> 87.6 us
  starting transfers between devices: 0 us -> 6.52 us
  waiting for transfers between devices: 0 us -> 4.82 us
  other arithmetic: 0 us -> 1.73 us
    pallas_call x1, Pallas kernels: 87.5 us -> 74.3 us  [run_power(): pl.pallas_call(functools.partial(power_kernel, sizes, vocab), out_shape=(...]
    ppermute x0 -> x2, starting transfers between devices: none -> 6.52 us  [the longest x1 5.22 us: on_device(): lax.ppermute(base_own, 'shard', [(i, i + 1) for i in range(shards - 1)])]
    ppermute x0 -> x2, waiting for transfers between devices: none -> 4.82 us  [the longest x1 4.15 us: on_device(): lax.ppermute(base_own, 'shard', [(i + 1, i) for i in range(shards - 1)])]
    pallas_call x1, Pallas kernels: 10.8 us -> 8.9 us  [run_update(): pl.pallas_call(functools.partial(update_kernel, entries), grid=(shards *...]
    convert_element_type x0 -> x1, other arithmetic: none -> 1.73 us  [on_device(): (master[0] - learn_rate * momentum_decay * momentum[0]).astype(bf16)]
    unnamed x26 -> x22, local copies, waits for them, and re-layouts: 3.99 us -> 3.99 us
  transfers between devices with their start and end apart: 0 -> 2, of which waited for: 0 -> 2; matrix products, arithmetic and copies ran while one was open for 0% -> 8% of each run, Pallas kernels for 0% -> 0%
where the time goes in v4:
time: 115 us
  Pallas kernels  87.6 us (76%)
  matrix products  9.14 us (8%)
  starting transfers between devices  6.52 us (6%)
  waiting for transfers between devices  4.82 us (4%)
  local copies, waits for them, and re-layouts  3.99 us (3%)
  other arithmetic  1.73 us (2%)
    pallas_call x1, Pallas kernels, run_power(): pl.pallas_call(functools.partial(power_kernel, sizes, vocab), out_shape=(...  74.3 us
    dot_general x1, matrix products, on_device(): lax.dot_general(out_grads[0], hidden_acts[0], (((0,), (0,)), ((), ())), p...  9.14 us
    pallas_call x1, Pallas kernels, run_update(): pl.pallas_call(functools.partial(update_kernel, entries), grid=(shards *...  8.9 us
    ppermute x1, starting transfers between devices, on_device(): lax.ppermute(base_own, 'shard', [(i, i + 1) for i in range(shards - 1)])  5.22 us
    pallas_call x1, Pallas kernels, run_table(): pl.pallas_call(table_kernel, grid=(table.shape[0] // count,), out_shape=j...  4.44 us
    ppermute x1, waiting for transfers between devices, on_device(): lax.ppermute(base_own, 'shard', [(i + 1, i) for i in range(shards - 1)])  4.15 us
    unnamed x22, local copies, waits for them, and re-layouts  3.99 us
  transfers between devices with their start and end apart: 2, of which 2 were waited for; matrix products, arithmetic and copies ran while one was open for 8% of the time, Pallas kernels for 0%

profile of v4, /device:TPU:0, one launch (start us, length us, event | category | flops | bytes accessed | tf_op | source)
XLA Modules:
  0.0 114.6 jit_solution(16313149800064608818)
XLA Ops:
  0.6 1.7 %subtract_convert_fusion = bf16[256,1024]{1,0:T(8,128)(2,1)S(1)} fusion(f32[1,256,1024]{2,1,0:T(8,128)} %param.15, f32[1,256,1024]{2,1,0:T(8,128)} %param.16), kind=kLoop, calls=%fused_computation.4 | loop fusion | flops 786432 | bytes 2621440 | tf_op jit(solution)/shard_map/convert_element_type | solution.py:514
  2.4 0.0 copy-start
  2.4 0.0 copy-start.5
  2.4 0.0 copy-start.7
  2.4 0.0 copy-start.8
  2.4 0.0 copy-start.10
  2.4 5.2 %collective-permute-start = (bf16[256,1024]{1,0:T(8,128)(2,1)S(1)}, bf16[256,1024]{1,0:T(8,128)(2,1)S(1)}, u32[]{:S(2)}, u32[]{:S(2)}) collective-permute-start(bf16[256,1024]{1,0:T(8,128)(2,1)S(1)} %subtract_convert_fusion), channel_id=1, source_target_pairs={{0,8},{8,16},{16,24},{1,9},{9,17},{17,25},{2,10},{10,18},{18,26},{... | collective-permute-start | bytes 1572872 | tf_op jit(solution)/shard_map/ppermute | solution.py:515
  7.7 1.3 %collective-permute-start.1 = (bf16[256,1024]{1,0:T(8,128)(2,1)S(1)}, bf16[256,1024]{1,0:T(8,128)(2,1)S(1)}, u32[]{:S(2)}, u32[]{:S(2)}) collective-permute-start(bf16[256,1024]{1,0:T(8,128)(2,1)S(1)} %subtract_convert_fusion), channel_id=1, source_target_pairs={{8,0},{16,8},{24,16},{9,1},{17,9},{25,17},{10,2},{18,10},{26,18},{... | collective-permute-start | bytes 1572872 | tf_op jit(solution)/shard_map/ppermute | solution.py:516
  9.0 9.1 %fusion.3.grad_ref = bf16[1024,1024]{1,0:T(8,128)(2,1)S(1)} fusion(bf16[1,2560,1024]{2,1,0:T(8,128)(2,1)} %param.10, bf16[1,2560,1024]{2,1,0:T(8,128)(2,1)} %param.11), kind=kOutput, calls=%fused_computation.3 | convolution fusion | flops 5369757696 | bytes 12582912 | tf_op jit(solution)/shard_map/dot_general | solution.py:517
  18.1 0.0 copy-start.1
  18.1 0.7 collective-permute-done.below_ref
  18.8 4.1 %collective-permute-done.1.above_ref = bf16[256,1024]{1,0:T(8,128)(2,1)S(1)} collective-permute-done((bf16[256,1024]{1,0:T(8,128)(2,1)S(1)}, bf16[256,1024]{1,0:T(8,128)(2,1)S(1)}, u32[]{:S(2)}, u32[]{:S(2)}) %collective-permute-start.1) | collective-permute-done | bytes 524320 | tf_op jit(solution)/shard_map/ppermute | solution.py:516
  22.9 0.0 copy-done
  22.9 0.0 copy-done.5
  22.9 0.0 copy-done.7
  23.0 74.3 %power_rounds.1 = (bf16[1024,96]{1,0:T(8,128)(2,1)S(1)}, f32[32,1024]{1,0:T(8,128)S(1)}, f32[8,128]{1,0:T(8,128)S(1)}, bf16[8,32,384]{2,1,0:T(8,128)(2,1)S(1)}, bf16[4,256,1024]{2,1,0:T(8,128)(2,1)S(1)}) custom-call(bf16[1024,1024]{1,0:T(8,128)(2,1)S(1)} %fusion.3.grad_ref, f32[1024,1024]{1,0:T(8,128)S(1)} %bitcast.26, f32[32,1024]{1,0:T(8,128)S(1)} %bitcast.29, ...), custom_call_target="tpu_custom_call" | custom-call | flops 1000000000 | bytes 120000000 | tf_op jit(solution)/shard_map/power_rounds/pallas_call | solution.py:355
  97.3 1.3 %copy-done.2 = bf16[4,256,1024]{2,1,0:T(8,128)(2,1)} copy-done((bf16[4,256,1024]{2,1,0:T(8,128)(2,1)}, bf16[4,256,1024]{2,1,0:T(8,128)(2,1)S(1)}, u32[]{:S(2)}) %copy-start.2) | copy-done | bytes 2097176
  98.6 0.7 copy-done.3
  99.3 0.7 copy-done.4
  100.0 0.7 copy-done.6
  100.6 0.6 copy-done.9
  101.2 4.4 %table_update.1 = bf16[4096,256]{1,0:T(8,128)(2,1)} custom-call(bf16[256,384]{1,0:T(8,128)(2,1)} %bitcast.28, bf16[4096,256]{1,0:T(8,128)(2,1)} %table_ref.1), custom_call_target="tpu_custom_call" | custom-call | tf_op jit(solution)/shard_map/table_update/pallas_call | solution.py:494
  105.7 0.0 copy-done.1
  105.7 8.9 %apply_update.1 = (f32[1024,1024]{1,0:T(8,128)}, f32[32,1024]{1,0:T(8,128)}, f32[256,1024]{1,0:T(8,128)}, f32[256,1024]{1,0:T(8,128)}, bf16[1024,1024]{1,0:T(8,128)(2,1)}) custom-call(bf16[1024,1024]{1,0:T(8,128)(2,1)} %copy-done.1, f32[1024,1024]{1,0:T(8,128)} %bitcast.25, bf16[1024,96]{1,0:T(8,128)(2,1)} %copy-done.3, f32[32,1024]{1,0:T(8,128)} %copy-done.6, ...), custom_call_target="tpu_custom_call" | custom-call | tf_op jit(solution)/shard_map/apply_update/pallas_call | solution.py:449
  (7 shorter events, 0.0 us)
Async XLA Ops:
  2.4 20.6 %copy-start = (f32[1,1,1024,1024]{3,2,1,0:T(8,128)S(1)}, f32[1,1,1024,1024]{3,2,1,0:T(8,128)}, u32[]{:S(2)}) copy-start(f32[1,1,1024,1024]{3,2,1,0:T(8,128)} %param.12) | copy-start | bytes 12582916
  2.4 20.6 %copy-start.5 = (f32[1,32,1024]{2,1,0:T(8,128)S(1)}, f32[1,32,1024]{2,1,0:T(8,128)}, u32[]{:S(2)}) copy-start(f32[1,32,1024]{2,1,0:T(8,128)} %param.13) | copy-start | bytes 393220
  2.4 20.6 %copy-start.7 = (bf16[128,256]{1,0:T(8,128)(2,1)S(1)}, bf16[128,256]{1,0:T(8,128)(2,1)}, u32[]{:S(2)}) copy-start(bf16[128,256]{1,0:T(8,128)(2,1)} %touched_ref.1) | copy-start | bytes 196612
  2.4 20.5 %copy-start.8 = (f32[1,2,32,32]{3,2,1,0:T(8,128)S(1)}, f32[1,2,32,32]{3,2,1,0:T(8,128)}, u32[]{:S(2)}) copy-start(f32[1,2,32,32]{3,2,1,0:T(8,128)} %param.14) | copy-start | bytes 24580
  2.4 20.5 %copy-start.10 = (s32[128]{0:T(128)S(1)}, s32[128]{0:T(128)}, u32[]{:S(2)}) copy-start(s32[128]{0:T(128)} %param.18) | copy-start | bytes 1540
  2.4 16.4 %collective-permute-start = (bf16[256,1024]{1,0:T(8,128)(2,1)S(1)}, bf16[256,1024]{1,0:T(8,128)(2,1)S(1)}, u32[]{:S(2)}, u32[]{:S(2)}) collective-permute-start(bf16[256,1024]{1,0:T(8,128)(2,1)S(1)} %subtract_convert_fusion), channel_id=1, source_target_pairs={{0,8},{8,16},{16,24},{1,9},{9,17},{17,25},{2,10},{10,18},{18,26},{... | collective-permute-start | bytes 1572872 | tf_op jit(solution)/shard_map/ppermute | solution.py:515
  7.7 15.3 %collective-permute-start.1 = (bf16[256,1024]{1,0:T(8,128)(2,1)S(1)}, bf16[256,1024]{1,0:T(8,128)(2,1)S(1)}, u32[]{:S(2)}, u32[]{:S(2)}) collective-permute-start(bf16[256,1024]{1,0:T(8,128)(2,1)S(1)} %subtract_convert_fusion), channel_id=1, source_target_pairs={{8,0},{16,8},{24,16},{9,1},{17,9},{25,17},{10,2},{18,10},{26,18},{... | collective-permute-start | bytes 1572872 | tf_op jit(solution)/shard_map/ppermute | solution.py:516
  18.1 87.6 %copy-start.1 = (bf16[1024,1024]{1,0:T(8,128)(2,1)}, bf16[1024,1024]{1,0:T(8,128)(2,1)S(1)}, u32[]{:S(2)}) copy-start(bf16[1024,1024]{1,0:T(8,128)(2,1)S(1)} %fusion.3.grad_ref) | copy-start | bytes 6291460
  97.3 1.3 %copy-start.2 = (bf16[4,256,1024]{2,1,0:T(8,128)(2,1)}, bf16[4,256,1024]{2,1,0:T(8,128)(2,1)S(1)}, u32[]{:S(2)}) copy-start(bf16[4,256,1024]{2,1,0:T(8,128)(2,1)S(1)} %get-tuple-element.19) | copy-start | bytes 6291460
  98.6 0.7 copy-start.3
  99.3 0.7 copy-start.4
  100.0 0.7 copy-start.6
  100.6 0.6 copy-start.9

commit v5 on v4

--- a/solution.py
+++ b/solution.py
@@ -211,9 +211,14 @@
     low_ref[...] = low
 
     def exchange(count, copy):
-        @pl.loop(1, count)
-        def _(k):
-            copy(k).start()
+        if count <= 16:
+            for k in range(1, count):
+                copy(k).start()
+        else:
+
+            @pl.loop(1, count)
+            def _(k):
+                copy(k).start()
 
         @pl.loop(1, count)
         def _(k):

time: 115 us -> 115 us (level)
  no operation moved by 1% of the time
where the time goes in v5:
time: 115 us
  Pallas kernels  87.6 us (76%)
  matrix products  9.14 us (8%)
  starting transfers between devices  6.52 us (6%)
  waiting for transfers between devices  4.82 us (4%)
  local copies, waits for them, and re-layouts  3.99 us (3%)
  other arithmetic  1.73 us (2%)
    pallas_call x1, Pallas kernels, run_power(): pl.pallas_call(functools.partial(power_kernel, sizes, vocab), out_shape=(...  74.2 us
    dot_general x1, matrix products, on_device(): lax.dot_general(out_grads[0], hidden_acts[0], (((0,), (0,)), ((), ())), p...  9.14 us
    pallas_call x1, Pallas kernels, run_update(): pl.pallas_call(functools.partial(update_kernel, entries), grid=(shards *...  8.9 us
    ppermute x1, starting transfers between devices, on_device(): lax.ppermute(base_own, 'shard', [(i, i + 1) for i in range(shards - 1)])  5.22 us
    pallas_call x1, Pallas kernels, run_table(): pl.pallas_call(table_kernel, grid=(table.shape[0] // count,), out_shape=j...  4.44 us
    ppermute x1, waiting for transfers between devices, on_device(): lax.ppermute(base_own, 'shard', [(i + 1, i) for i in range(shards - 1)])  4.15 us
    unnamed x22, local copies, waits for them, and re-layouts  3.99 us
  transfers between devices with their start and end apart: 2, of which 2 were waited for; matrix products, arithmetic and copies ran while one was open for 8% of the time, Pallas kernels for 0%

profile of v5, /device:TPU:0, one launch (start us, length us, event | category | flops | bytes accessed | tf_op | source)
XLA Modules:
  0.0 114.5 jit_solution(15387578469878070618)
XLA Ops:
  0.6 1.7 %subtract_convert_fusion = bf16[256,1024]{1,0:T(8,128)(2,1)S(1)} fusion(f32[1,256,1024]{2,1,0:T(8,128)} %param.15, f32[1,256,1024]{2,1,0:T(8,128)} %param.16), kind=kLoop, calls=%fused_computation.4 | loop fusion | flops 786432 | bytes 2621440 | tf_op jit(solution)/shard_map/convert_element_type | solution.py:519
  2.4 0.0 copy-start
  2.4 0.0 copy-start.5
  2.4 0.0 copy-start.7
  2.4 0.0 copy-start.8
  2.4 0.0 copy-start.10
  2.4 5.2 %collective-permute-start = (bf16[256,1024]{1,0:T(8,128)(2,1)S(1)}, bf16[256,1024]{1,0:T(8,128)(2,1)S(1)}, u32[]{:S(2)}, u32[]{:S(2)}) collective-permute-start(bf16[256,1024]{1,0:T(8,128)(2,1)S(1)} %subtract_convert_fusion), channel_id=1, source_target_pairs={{0,8},{8,16},{16,24},{1,9},{9,17},{17,25},{2,10},{10,18},{18,26},{... | collective-permute-start | bytes 1572872 | tf_op jit(solution)/shard_map/ppermute | solution.py:520
  7.7 1.3 %collective-permute-start.1 = (bf16[256,1024]{1,0:T(8,128)(2,1)S(1)}, bf16[256,1024]{1,0:T(8,128)(2,1)S(1)}, u32[]{:S(2)}, u32[]{:S(2)}) collective-permute-start(bf16[256,1024]{1,0:T(8,128)(2,1)S(1)} %subtract_convert_fusion), channel_id=1, source_target_pairs={{8,0},{16,8},{24,16},{9,1},{17,9},{25,17},{10,2},{18,10},{26,18},{... | collective-permute-start | bytes 1572872 | tf_op jit(solution)/shard_map/ppermute | solution.py:521
  9.0 9.1 %fusion.3.grad_ref = bf16[1024,1024]{1,0:T(8,128)(2,1)S(1)} fusion(bf16[1,2560,1024]{2,1,0:T(8,128)(2,1)} %param.10, bf16[1,2560,1024]{2,1,0:T(8,128)(2,1)} %param.11), kind=kOutput, calls=%fused_computation.3 | convolution fusion | flops 5369757696 | bytes 12582912 | tf_op jit(solution)/shard_map/dot_general | solution.py:522
  18.1 0.0 copy-start.1
  18.1 0.7 collective-permute-done.below_ref
  18.8 4.1 %collective-permute-done.1.above_ref = bf16[256,1024]{1,0:T(8,128)(2,1)S(1)} collective-permute-done((bf16[256,1024]{1,0:T(8,128)(2,1)S(1)}, bf16[256,1024]{1,0:T(8,128)(2,1)S(1)}, u32[]{:S(2)}, u32[]{:S(2)}) %collective-permute-start.1) | collective-permute-done | bytes 524320 | tf_op jit(solution)/shard_map/ppermute | solution.py:521
  22.9 0.0 copy-done
  22.9 0.0 copy-done.5
  22.9 0.0 copy-done.7
  23.0 74.2 %power_rounds.1 = (bf16[1024,96]{1,0:T(8,128)(2,1)S(1)}, f32[32,1024]{1,0:T(8,128)S(1)}, f32[8,128]{1,0:T(8,128)S(1)}, bf16[8,32,384]{2,1,0:T(8,128)(2,1)S(1)}, bf16[4,256,1024]{2,1,0:T(8,128)(2,1)S(1)}) custom-call(bf16[1024,1024]{1,0:T(8,128)(2,1)S(1)} %fusion.3.grad_ref, f32[1024,1024]{1,0:T(8,128)S(1)} %bitcast.26, f32[32,1024]{1,0:T(8,128)S(1)} %bitcast.29, ...), custom_call_target="tpu_custom_call" | custom-call | flops 1000000000 | bytes 120000000 | tf_op jit(solution)/shard_map/power_rounds/pallas_call | solution.py:360
  97.2 1.3 %copy-done.2 = bf16[4,256,1024]{2,1,0:T(8,128)(2,1)} copy-done((bf16[4,256,1024]{2,1,0:T(8,128)(2,1)}, bf16[4,256,1024]{2,1,0:T(8,128)(2,1)S(1)}, u32[]{:S(2)}) %copy-start.2) | copy-done | bytes 2097176
  98.5 0.7 copy-done.3
  99.2 0.7 copy-done.4
  99.9 0.7 copy-done.6
  100.6 0.6 copy-done.9
  101.2 4.4 %table_update.1 = bf16[4096,256]{1,0:T(8,128)(2,1)} custom-call(bf16[256,384]{1,0:T(8,128)(2,1)} %bitcast.28, bf16[4096,256]{1,0:T(8,128)(2,1)} %table_ref.1), custom_call_target="tpu_custom_call" | custom-call | tf_op jit(solution)/shard_map/table_update/pallas_call | solution.py:499
  105.6 0.0 copy-done.1
  105.6 8.9 %apply_update.1 = (f32[1024,1024]{1,0:T(8,128)}, f32[32,1024]{1,0:T(8,128)}, f32[256,1024]{1,0:T(8,128)}, f32[256,1024]{1,0:T(8,128)}, bf16[1024,1024]{1,0:T(8,128)(2,1)}) custom-call(bf16[1024,1024]{1,0:T(8,128)(2,1)} %copy-done.1, f32[1024,1024]{1,0:T(8,128)} %bitcast.25, bf16[1024,96]{1,0:T(8,128)(2,1)} %copy-done.3, f32[32,1024]{1,0:T(8,128)} %copy-done.6, ...), custom_call_target="tpu_custom_call" | custom-call | tf_op jit(solution)/shard_map/apply_update/pallas_call | solution.py:454
  (7 shorter events, 0.0 us)
Async XLA Ops:
  2.4 20.6 %copy-start = (f32[1,1,1024,1024]{3,2,1,0:T(8,128)S(1)}, f32[1,1,1024,1024]{3,2,1,0:T(8,128)}, u32[]{:S(2)}) copy-start(f32[1,1,1024,1024]{3,2,1,0:T(8,128)} %param.12) | copy-start | bytes 12582916
  2.4 20.6 %copy-start.5 = (f32[1,32,1024]{2,1,0:T(8,128)S(1)}, f32[1,32,1024]{2,1,0:T(8,128)}, u32[]{:S(2)}) copy-start(f32[1,32,1024]{2,1,0:T(8,128)} %param.13) | copy-start | bytes 393220
  2.4 20.6 %copy-start.7 = (bf16[128,256]{1,0:T(8,128)(2,1)S(1)}, bf16[128,256]{1,0:T(8,128)(2,1)}, u32[]{:S(2)}) copy-start(bf16[128,256]{1,0:T(8,128)(2,1)} %touched_ref.1) | copy-start | bytes 196612
  2.4 20.5 %copy-start.8 = (f32[1,2,32,32]{3,2,1,0:T(8,128)S(1)}, f32[1,2,32,32]{3,2,1,0:T(8,128)}, u32[]{:S(2)}) copy-start(f32[1,2,32,32]{3,2,1,0:T(8,128)} %param.14) | copy-start | bytes 24580
  2.4 20.5 %copy-start.10 = (s32[128]{0:T(128)S(1)}, s32[128]{0:T(128)}, u32[]{:S(2)}) copy-start(s32[128]{0:T(128)} %param.18) | copy-start | bytes 1540
  2.4 16.4 %collective-permute-start = (bf16[256,1024]{1,0:T(8,128)(2,1)S(1)}, bf16[256,1024]{1,0:T(8,128)(2,1)S(1)}, u32[]{:S(2)}, u32[]{:S(2)}) collective-permute-start(bf16[256,1024]{1,0:T(8,128)(2,1)S(1)} %subtract_convert_fusion), channel_id=1, source_target_pairs={{0,8},{8,16},{16,24},{1,9},{9,17},{17,25},{2,10},{10,18},{18,26},{... | collective-permute-start | bytes 1572872 | tf_op jit(solution)/shard_map/ppermute | solution.py:520
  7.7 15.3 %collective-permute-start.1 = (bf16[256,1024]{1,0:T(8,128)(2,1)S(1)}, bf16[256,1024]{1,0:T(8,128)(2,1)S(1)}, u32[]{:S(2)}, u32[]{:S(2)}) collective-permute-start(bf16[256,1024]{1,0:T(8,128)(2,1)S(1)} %subtract_convert_fusion), channel_id=1, source_target_pairs={{8,0},{16,8},{24,16},{9,1},{17,9},{25,17},{10,2},{18,10},{26,18},{... | collective-permute-start | bytes 1572872 | tf_op jit(solution)/shard_map/ppermute | solution.py:521
  18.1 87.5 %copy-start.1 = (bf16[1024,1024]{1,0:T(8,128)(2,1)}, bf16[1024,1024]{1,0:T(8,128)(2,1)S(1)}, u32[]{:S(2)}) copy-start(bf16[1024,1024]{1,0:T(8,128)(2,1)S(1)} %fusion.3.grad_ref) | copy-start | bytes 6291460
  97.2 1.3 %copy-start.2 = (bf16[4,256,1024]{2,1,0:T(8,128)(2,1)}, bf16[4,256,1024]{2,1,0:T(8,128)(2,1)S(1)}, u32[]{:S(2)}) copy-start(bf16[4,256,1024]{2,1,0:T(8,128)(2,1)S(1)} %get-tuple-element.19) | copy-start | bytes 6291460
  98.5 0.7 copy-start.3
  99.2 0.7 copy-start.4
  99.9 0.7 copy-start.6
  100.6 0.6 copy-start.9
